TPU v7x, 32 devices: a whole 2x2x4 slice. The times are simulated.
32 devices in a mesh: dp: 4 (over y, x), section: 2 (over core), tensor: 4 (over z).
Axes of the slice: x: 2, y: 2, z: 4, core: 2. Of those that a mesh axis runs over, the one named last changes fastest.
Arguments:
- stored: bfloat16 [2, 2, 256, 8192], P('section', None, 'dp', 'tensor'), may hold values from -6 to 6
- cotangent: bfloat16 [2, 32, 8192], P(None, None, 'tensor'), may hold values from -12 to 12
- positions: int32 [2, 32], replicated, may hold values from 128 to 255, as said below
- lengths: int32 [2], replicated, may hold values from 128 to 256, as said below
- norm_gain: float32 [2, 8192], P('section'), may hold values from 0.5 to 1.5
- w_query: bfloat16 [2, 8192, 8192], P('section', None, 'tensor')
- w_key: bfloat16 [2, 8192, 1024], P('section', None, 'tensor')
- w_value: bfloat16 [2, 8192, 1024], P('section', None, 'tensor'), may hold values from -0.0625 to 0.0625
- w_out: bfloat16 [2, 8192, 8192], P('section', 'tensor', 'dp'), may hold values from -0.0625 to 0.0625
Outputs:
- input_grads: float32 [2, 2, 256, 8192], P('section', None, 'dp', 'tensor')
Inputs may be any that keep to these rules, and one draw needn't show every extreme that they name: In each sequence the response positions are distinct, rise along the last dimension, lie in the last 128 positions, and the last one is 255. `lengths`: some sequence has length 256.
All inputs are finite; a program needn't handle non-finite values.
Results may differ from a plain program's by a relative error of at most 0.017.
Values may be sent and summed in bfloat16 or wider, within the bound.
A program may use at most 256 MiB of HBM per device.

v0:
```python
import math

import jax
import jax.numpy as jnp
from jax import lax
from jax.sharding import PartitionSpec as P

HD = 128


EPS = 1e-05
THETA = 500000.0


def passed_along(value, axis, steps):
    count = lax.axis_size(axis)
    leading, last = (max(0, -steps), min(count, count - steps))
    return lax.ppermute(value, axis, [(source, source + steps) for source in range(leading, last)])


def angle_tables(row_places):
    half_dim = HD // 2
    frequency = THETA ** (-(jnp.arange(half_dim, dtype=jnp.float32) * 2.0) / HD)
    angles = row_places[:, None] * frequency[None, :]
    cosine = jnp.concatenate([jnp.cos(angles), jnp.cos(angles)], -1)[:, None, :]
    sine_table = jnp.concatenate([jnp.sin(angles), jnp.sin(angles)], -1)[:, None, :]
    return (cosine, sine_table)


def turn_half(values):
    half_dim = values.shape[-1] // 2
    return jnp.concatenate([-values[..., half_dim:], values[..., :half_dim]], -1)


def rotate(values, cosine, sine_table):
    return values * cosine + turn_half(values) * sine_table


def unrotate(values, cosine, sine_table):
    return values * cosine - turn_half(values * sine_table)


def layer_grad(own_input, own_upstream, seq_lengths, gain, w_query, w_key, w_value, w_out):
    batch, rows, width_dev = own_input.shape
    kv_dev = w_key.shape[1] // HD
    q_dev = w_query.shape[1] // HD
    group = q_dev // kv_dev
    scale = 1.0 / math.sqrt(HD)
    x_whole, g_whole = (
        lax.all_gather(own_input, "tensor", axis=2, tiled=True),
        lax.all_gather(own_upstream, "tensor", axis=2, tiled=True),
    )
    width = x_whole.shape[2]
    x_full = x_whole.astype(jnp.float32)
    inv_rms = lax.rsqrt(jnp.mean(x_full * x_full, -1, keepdims=True) + EPS)
    normed = (x_full * inv_rms * gain).astype(jnp.bfloat16)
    first_row = lax.axis_index("dp") * rows
    query_ids = first_row + jnp.arange(rows, dtype=jnp.int32)
    cosine, sine_table = angle_tables(query_ids.astype(jnp.float32))
    queries = jnp.einsum(
        "bpd,dc->bpc", normed, w_query, preferred_element_type=jnp.float32
    ).reshape(batch, rows, q_dev, HD)
    keys = jnp.einsum("bpd,dc->bpc", normed, w_key, preferred_element_type=jnp.float32).reshape(
        batch, rows, kv_dev, HD
    )
    values = jnp.einsum("bpd,dc->bpc", normed, w_value, preferred_element_type=jnp.float32).reshape(
        batch, rows, kv_dev, HD
    )
    q_rot = rotate(queries, cosine, sine_table).astype(jnp.bfloat16)
    k_rot = rotate(keys, cosine, sine_table).astype(jnp.bfloat16)
    values_b = values.astype(jnp.bfloat16)
    grad_out = jnp.einsum("bpd,cd->bpc", g_whole, w_out, preferred_element_type=jnp.float32).astype(
        jnp.bfloat16
    )
    all_keys, all_values = (
        lax.all_gather(k_rot, "dp", axis=1, tiled=True),
        lax.all_gather(values_b, "dp", axis=1, tiled=True),
    )
    length = all_keys.shape[1]
    q_five = q_rot.reshape(batch, rows, kv_dev, group, HD)
    o_five = grad_out.reshape(batch, rows, kv_dev, group, HD)
    key_ids = jnp.arange(length, dtype=jnp.int32)
    causal = key_ids[None, None, :] <= query_ids[None, :, None]
    start_pos = length - seq_lengths
    inside = (key_ids[None, None, :] >= start_pos[:, None, None]) | (
        key_ids[None, None, :] == query_ids[None, :, None]
    )
    allowed = (causal & inside)[:, None, None, :, :]
    scores = (
        jnp.einsum("bpkgd,bjkd->bkgpj", q_five, all_keys, preferred_element_type=jnp.float32)
        * scale
    )
    masked = jnp.where(allowed, scores, -1e30)
    highest = jnp.max(masked, -1, keepdims=True)
    expo_terms = jnp.where(allowed, jnp.exp(masked - highest), 0.0)
    probs = expo_terms / jnp.sum(expo_terms, -1, keepdims=True)
    grad_probs = jnp.einsum(
        "bpkgd,bjkd->bkgpj", o_five, all_values, preferred_element_type=jnp.float32
    )
    row_dot = jnp.sum(probs * grad_probs, -1, keepdims=True)
    grad_scores = (probs * (grad_probs - row_dot) * scale).astype(jnp.bfloat16)
    probs_b = probs.astype(jnp.bfloat16)
    grad_qr = jnp.einsum(
        "bkgpj,bjkd->bpkgd", grad_scores, all_keys, preferred_element_type=jnp.float32
    )
    key_terms = jnp.einsum(
        "bkgpj,bpkgd->bjkd", grad_scores, q_five, preferred_element_type=jnp.float32
    )
    value_terms = jnp.einsum(
        "bkgpj,bpkgd->bjkd", probs_b, o_five, preferred_element_type=jnp.float32
    )
    grad_kr, grad_vr = (
        lax.psum_scatter(
            key_terms.astype(jnp.bfloat16), "dp", scatter_dimension=1, tiled=True
        ).astype(jnp.float32),
        lax.psum_scatter(
            value_terms.astype(jnp.bfloat16), "dp", scatter_dimension=1, tiled=True
        ).astype(jnp.float32),
    )
    grad_q = (
        unrotate(grad_qr.reshape(batch, rows, q_dev, HD), cosine, sine_table)
        .astype(jnp.bfloat16)
        .reshape(batch, rows, q_dev * HD)
    )
    grad_k = (
        unrotate(grad_kr, cosine, sine_table).astype(jnp.bfloat16).reshape(batch, rows, kv_dev * HD)
    )
    grad_v = grad_vr.astype(jnp.bfloat16).reshape(batch, rows, kv_dev * HD)
    partial_term = jnp.einsum("bpc,dc->bpd", grad_q, w_query, preferred_element_type=jnp.float32)
    partial_term = partial_term + jnp.einsum(
        "bpc,dc->bpd", grad_k, w_key, preferred_element_type=jnp.float32
    )
    partial_term = partial_term + jnp.einsum(
        "bpc,dc->bpd", grad_v, w_value, preferred_element_type=jnp.float32
    )
    summed = lax.psum(partial_term.astype(jnp.bfloat16), "tensor").astype(jnp.float32)
    stat = jnp.sum(x_full * gain * summed, -1, keepdims=True)
    whole_grad = (
        g_whole.astype(jnp.float32) + inv_rms * gain * summed - x_full * inv_rms**3 * stat / width
    )
    return lax.dynamic_slice_in_dim(whole_grad, lax.axis_index("tensor") * width_dev, width_dev, 2)


def on_device(stored, cotangent, positions, lengths, norm_gain, w_query, w_key, w_value, w_out):
    own_input = stored[0]
    gain = norm_gain[0]
    wq_layer = w_query[0]
    wk_layer = w_key[0]
    wv_layer = w_value[0]
    wo_layer = lax.all_gather(w_out[0], "dp", axis=1, tiled=True)
    seqs, rows, width_dev = own_input.shape
    section_id = lax.axis_index("section")
    row_ids = lax.axis_index("dp") * rows + jnp.arange(rows, dtype=jnp.int32)
    placed = (positions[:, None, :] == row_ids[None, :, None]).astype(jnp.bfloat16)
    from_loss = jnp.einsum(
        "spr,srd->spd", placed, cotangent, preferred_element_type=jnp.float32
    ).astype(jnp.bfloat16)

    def run_layer(input_part, upstream_part, length_part):
        return layer_grad(
            input_part, upstream_part, length_part, gain, wq_layer, wk_layer, wv_layer, wo_layer
        )

    first_in = jnp.where(section_id == 1, from_loss, jnp.zeros_like(from_loss))
    first_pass = run_layer(own_input, first_in, lengths)
    handed = passed_along(first_pass.astype(jnp.bfloat16), "section", -1)
    second_pass = run_layer(own_input, handed, lengths)
    result = jnp.where(section_id == 0, second_pass, first_pass)
    return result[None]


def solution(mesh):
    return jax.shard_map(
        on_device,
        mesh=mesh,
        in_specs=(
            P("section", None, "dp", "tensor"),
            P(None, None, "tensor"),
            P(),
            P(),
            P("section", None),
            P("section", None, "tensor"),
            P("section", None, "tensor"),
            P("section", None, "tensor"),
            P("section", "tensor", "dp"),
        ),
        out_specs=P("section", None, "dp", "tensor"),
        check_vma=False,
    )
```

profile of v0, /device:TPU:0, one launch (start us, length us, event | category | flops | bytes accessed | tf_op | source)
XLA Modules:
  0.0 915.4 jit_solution(1680415631563956756)
XLA Ops:
  6.5 0.7 all-gather.11.cloned.1.call-update
  7.5 2.0 fusion.50
  9.5 0.7 all-gather.13.cloned.1.call-update
  10.3 40.0 %copy.63 = bf16[2048,8192]{1,0:T(8,128)(2,1)} copy(bf16[2048,8192]{0,1:T(8,128)(2,1)} %bitcast.235) | data formatting | bytes 67108864 | tf_op jit(solution)/shard_map/bpd,dc->bpc/dot_general | solution.py:60
  50.3 6.4 copy.62
  56.7 6.4 copy.64
  63.1 0.6 dynamic-slice
  64.9 2.3 fusion.33
  67.4 3.9 fusion.117
  71.5 10.4 %all_gather.23 = bf16[2,256,2,128]{3,1,2,0:T(8,128)(2,1)S(1)} all-gather(bf16[2,64,2,128]{3,1,2,0:T(8,128)(2,1)S(1)} %fusion.113), channel_id=1, replica_groups=mesh['dp'=4,'section'=2,'tensor'=4] {'dp'}, dimensions={1}, use_global_device_ids=true | all-gather | bytes 327680 | tf_op jit(solution)/shard_map/all_gather | solution.py:76
  81.9 1.5 convolution_convert_fusion.1
  83.5 9.8 %all_gather.24 = bf16[2,256,2,128]{3,1,2,0:T(8,128)(2,1)S(1)} all-gather(bf16[2,64,2,128]{3,1,2,0:T(8,128)(2,1)S(1)} %convolution_convert_fusion.1), channel_id=1, replica_groups=mesh['dp'=4,'section'=2,'tensor'=4] {'dp'}, dimensions={1}, use_global_device_ids=true | all-gather | bytes 327680 | tf_op jit(solution)/shard_map/all_gather | solution.py:77
  93.3 15.8 %fusion.115 = f32[2,64,16,128]{3,1,2,0:T(8,128)S(1)} fusion(bf16[16,128,8192,1]{2,1,0,3:T(8,128)(2,1)} %bitcast.236, bf16[1,2,64,8192]{3,2,1,0:T(8,128)(2,1)S(1)} %copy-done.2, f32[8192]{0:T(1024)S(1)} %bitcast.253, f32[2,64]{1,0:T(2,128)S(1)} %get-tuple-element.23), kind=kOutput, calls=%fused_computation.131 | convolution fusion | flops 4299161600 | bytes 36733440 | tf_op jit(solution)/shard_map/bpd,dc->bpc/dot_general | solution.py:60
  109.1 0.4 slice_negate_fusion.2
  109.5 0.4 fusion.74
  109.9 2.2 fusion.146
  112.2 3.9 fusion.143
  116.0 285.7 %all-gather.13.cloned.1.call-done = bf16[1,2048,8192]{2,1,0:T(8,128)(2,1)} async-done(((bf16[1,2048,2048]{2,1,0:T(8,128)(2,1)}), bf16[1,2048,8192]{2,1,0:T(8,128)(2,1)}) %all-gather.13.cloned.1.call-update) | async-done | bytes 33554448 | tf_op jit(solution)/shard_map/all_gather | solution.py:150
  401.7 16.4 %fusion.44 = bf16[2,64,2048]{2,1,0:T(8,128)(2,1)S(1)} fusion(bf16[2,64,8192]{2,1,0:T(8,128)(2,1)} %all-gather.7.cloned.1.call-done, bf16[1,2048,8192]{2,1,0:T(8,128)(2,1)} %all-gather.13.cloned.1.call-done), kind=kOutput, calls=%fused_computation.36 | convolution fusion | flops 4295229440 | bytes 36175872 | tf_op jit(solution)/shard_map/bpd,cd->bpc/dot_general | solution.py:72
  418.2 0.8 copy-done.13
  419.0 1.7 fusion.96
  420.8 15.5 %fusion.77 = f32[2,2,128,8,64]{2,4,3,1,0:T(8,128)} fusion(f32[2,2,256,64,8]{2,3,4,1,0:T(8,128)} %fusion.96, bf16[2,256,2,128]{3,1,2,0:T(8,128)(2,1)S(1)} %all_gather.23, f32[2,2,8,64,256]{4,3,2,1,0:T(8,128)} %get-tuple-element.29, f32[2,2,8,64]{3,2,1,0:T(8,128)S(1)} %get-tuple-element.28), kind=kOutput, calls=%fused_computation.86 | convolution fusion | flops 137890048 | bytes 5513216 | tf_op jit(solution)/shard_map/bkgpj,bjkd->bpkgd/dot_general | solution.py:103
  436.3 1.4 broadcast_multiply_fusion.2
  437.7 0.3 copy-done.15
  438.0 1.5 fusion.65
  439.4 1.8 copy.45
  441.5 1.7 slice_negate_fusion.1
  443.2 16.2 %fusion.66 = bf16[2,256,2,128]{3,1,2,0:T(8,128)(2,1)} fusion(bf16[2,64,2,8,128]{4,1,3,2,0:T(8,128)(2,1)} %bitcast.257, f32[2,2,256,64,8]{2,3,4,1,0:T(8,128)} %fusion.96, f32[2,2,8,64,256]{4,3,2,1,0:T(8,128)} %get-tuple-element.29, f32[2,2,8,64]{3,2,1,0:T(8,128)S(1)} %get-tuple-element.28), kind=kOutput, calls=%fused_computation.66 | convolution fusion | flops 138021120 | bytes 4988928 | tf_op jit(solution)/shard_map/bkgpj,bpkgd->bjkd/dot_general | solution.py:106
  459.5 24.9 %all-reduce.11.cloned.1.call-done = bf16[2,256,2,128]{3,2,0,1:T(2,128)(2,1)} async-done(((bf16[2,256,2,128]{3,2,0,1:T(2,128)(2,1)}), bf16[2,256,2,128]{3,2,0,1:T(2,128)(2,1)}) %all-reduce.11.cloned.1.call-update) | async-done | bytes 262160
  484.5 0.9 constant_dynamic-slice_fusion.1
  485.4 5.8 fusion.38
  491.2 20.2 %reduce-scatter.3.cloned.1.call-done = bf16[2,64,2,128]{3,1,2,0:T(8,128)(2,1)} async-done(((bf16[2,256,2,128]{3,1,2,0:T(8,128)(2,1)}), bf16[2,64,2,128]{3,1,2,0:T(8,128)(2,1)}) %reduce-scatter.3.cloned.1.call-update) | async-done | bytes 65552 | tf_op jit(solution)/shard_map/reduce_scatter | solution.py:113
  511.4 0.9 convert_multiply_fusion.6
  512.4 5.8 fusion.42
  518.2 19.2 %fusion.26 = bf16[2,64,8192]{2,1,0:T(8,128)(2,1)} fusion(f32[2,64,8192]{2,1,0:T(8,128)} %fusion.38, f32[2,64,8192]{2,1,0:T(8,128)} %fusion.42, bf16[1,8192,2048]{2,1,0:T(8,128)(2,1)} %param.14, f32[2,64,16,64]{3,1,2,0:T(8,128)} %get-tuple-element.12, f32[2,64,16,64]{3,1,2,0:T(8,128)} %get-tuple-element.11, f32[2,64,16,128]{3,1,2,0:T(8,128)S(1)} %bitcast.242, ...), kind=kOutput, calls=%fused_computation.16 | convolution fusion | flops 4299161600 | bytes 46170112 | tf_op jit(solution)/shard_map/bpc,dc->bpd/dot_general | solution.py:129
  537.5 86.6 %all-reduce.7.cloned.1.call-done = bf16[2,64,8192]{2,1,0:T(8,128)(2,1)} async-done(((bf16[2,64,8192]{2,1,0:T(8,128)(2,1)}), bf16[2,64,8192]{2,1,0:T(8,128)(2,1)}) %all-reduce.7.cloned.1.call-update) | async-done | bytes 2097168 | tf_op jit(solution)/shard_map/psum | solution.py:136
  624.1 2.2 convert_element_type.155
  626.3 2.0 convert_multiply_fusion.1
  628.3 3.4 fusion.144
  631.9 1.3 collective-permute-start
  633.1 2.5 collective-permute-done
  635.7 0.8 copy-done.19
  636.8 44.8 %all-gather.9.cloned.1.call-done = bf16[2,64,8192]{2,1,0:T(8,128)(2,1)} async-done(((bf16[2,64,2048]{2,1,0:T(8,128)(2,1)}), bf16[2,64,8192]{2,1,0:T(8,128)(2,1)}) %all-gather.9.cloned.1.call-update) | async-done | bytes 2097168 | tf_op jit(solution)/shard_map/all_gather | solution.py:51
  681.5 16.4 %fusion.47 = bf16[2,64,2048]{2,1,0:T(8,128)(2,1)S(1)} fusion(bf16[2,64,8192]{2,1,0:T(8,128)(2,1)} %all-gather.9.cloned.1.call-done, bf16[1,2048,8192]{2,1,0:T(8,128)(2,1)} %all-gather.13.cloned.1.call-done), kind=kOutput, calls=%fused_computation.37 | convolution fusion | flops 4295229440 | bytes 36175872 | tf_op jit(solution)/shard_map/bpd,cd->bpc/dot_general | solution.py:72
  698.1 1.8 fusion.93
  699.8 1.5 fusion.63
  701.3 15.6 %fusion.79 = f32[2,2,128,8,64]{2,4,3,1,0:T(8,128)} fusion(f32[2,2,256,64,8]{2,3,4,1,0:T(8,128)} %fusion.93, bf16[2,256,2,128]{3,1,2,0:T(8,128)(2,1)S(1)} %copy-done.21, f32[2,2,8,64,256]{4,3,2,1,0:T(8,128)} %get-tuple-element.29, f32[2,2,8,64]{3,2,1,0:T(8,128)S(1)} %get-tuple-element.28), kind=kOutput, calls=%fused_computation.88 | convolution fusion | flops 137890048 | bytes 5513216 | tf_op jit(solution)/shard_map/bkgpj,bjkd->bpkgd/dot_general | solution.py:103
  716.9 1.3 broadcast_multiply_fusion.1
  718.2 1.8 copy.53
  720.1 1.8 slice_negate_fusion
  721.9 16.3 %fusion.64 = bf16[2,256,2,128]{3,1,2,0:T(8,128)(2,1)} fusion(bf16[2,64,2,8,128]{4,1,3,2,0:T(8,128)(2,1)} %bitcast.258, f32[2,2,256,64,8]{2,3,4,1,0:T(8,128)} %fusion.93, f32[2,2,8,64,256]{4,3,2,1,0:T(8,128)} %get-tuple-element.29, f32[2,2,8,64]{3,2,1,0:T(8,128)S(1)} %get-tuple-element.28), kind=kOutput, calls=%fused_computation.64 | convolution fusion | flops 138021120 | bytes 4988928 | tf_op jit(solution)/shard_map/bkgpj,bpkgd->bjkd/dot_general | solution.py:106
  738.3 0.3 all-reduce.9.cloned.1.call-start
  738.6 23.4 %all-reduce.13.cloned.1.call-done = bf16[2,256,2,128]{3,2,0,1:T(2,128)(2,1)} async-done(((bf16[2,256,2,128]{3,2,0,1:T(2,128)(2,1)}), bf16[2,256,2,128]{3,2,0,1:T(2,128)(2,1)}) %all-reduce.13.cloned.1.call-update) | async-done | bytes 262160
  762.0 0.9 constant_dynamic-slice_fusion
  762.9 5.6 fusion.36
  768.5 20.3 %reduce-scatter.5.cloned.1.call-done = bf16[2,64,2,128]{3,1,2,0:T(8,128)(2,1)} async-done(((bf16[2,256,2,128]{3,1,2,0:T(8,128)(2,1)}), bf16[2,64,2,128]{3,1,2,0:T(8,128)(2,1)}) %reduce-scatter.5.cloned.1.call-update) | async-done | bytes 65552 | tf_op jit(solution)/shard_map/reduce_scatter | solution.py:113
  788.9 0.9 convert_multiply_fusion.4
  789.9 5.8 fusion.40
  795.7 19.3 %fusion.23 = bf16[2,64,8192]{2,1,0:T(8,128)(2,1)} fusion(f32[2,64,8192]{2,1,0:T(8,128)} %fusion.36, f32[2,64,8192]{2,1,0:T(8,128)} %fusion.40, bf16[1,8192,2048]{2,1,0:T(8,128)(2,1)} %param.14, f32[2,64,16,64]{3,1,2,0:T(8,128)} %get-tuple-element.10, f32[2,64,16,64]{3,1,2,0:T(8,128)} %get-tuple-element.9, f32[2,64,16,128]{3,1,2,0:T(8,128)S(1)} %bitcast.240, ...), kind=kOutput, calls=%fused_computation.15 | convolution fusion | flops 4299161600 | bytes 46170112 | tf_op jit(solution)/shard_map/bpc,dc->bpd/dot_general | solution.py:129
  815.0 86.7 %all-reduce.9.cloned.1.call-done = bf16[2,64,8192]{2,1,0:T(8,128)(2,1)} async-done(((bf16[2,64,8192]{2,1,0:T(8,128)(2,1)}), bf16[2,64,8192]{2,1,0:T(8,128)(2,1)}) %all-reduce.9.cloned.1.call-update) | async-done | bytes 2097168 | tf_op jit(solution)/shard_map/psum | solution.py:136
  901.7 2.2 convert_element_type.169
  903.9 0.9 fusion.32
  904.8 0.3 copy-done.10
  905.1 3.1 fusion.70
  (81 shorter events, 2.7 us)
Async XLA Ops:
  6.5 1.0 copy-start
  6.5 58.4 %all-gather.11.cloned.1.call-start = ((), (), s32[]{:S(2)}) async-start(), calls=%async_computation.8 | async-start | bytes 2621440 | tf_op jit(solution)/shard_map/all_gather | solution.py:50
  7.3 108.8 %all-gather.7.cloned.1.call-start = ((), (), s32[]{:S(2)}) async-start(), calls=%async_computation.2 | async-start | bytes 2621440 | tf_op jit(solution)/shard_map/all_gather | solution.py:51
  9.5 392.3 %all-gather.13.cloned.1.call-start = ((), (), s32[]{:S(2)}) async-start(), calls=%async_computation.9 | async-start | bytes 41943040 | tf_op jit(solution)/shard_map/all_gather | solution.py:150
  10.2 474.3 %all-reduce.11.cloned.1.call-start = ((), (), s32[]{:S(2)}) async-start(), calls=%async_computation.10 | async-start | bytes 524288
  56.7 6.4 copy-start.23
  56.7 8.0 copy-start.22
  63.1 4.2 copy-start.17
  64.9 2.5 copy-start.2
  67.4 14.5 %copy-start.9 = (bf16[256,8192]{1,0:T(8,128)(2,1)S(1)}, bf16[256,8192]{1,0:T(8,128)(2,1)}, u32[]{:S(2)}) copy-start(bf16[256,8192]{1,0:T(8,128)(2,1)} %copy.64) | copy-start | bytes 12582916
  81.9 338.9 %copy-start.20 = (bf16[2,256,2,128]{3,1,2,0:T(8,128)(2,1)}, bf16[2,256,2,128]{3,1,2,0:T(8,128)(2,1)S(1)}, u32[]{:S(2)}) copy-start(bf16[2,256,2,128]{3,1,2,0:T(8,128)(2,1)S(1)} %all_gather.23) | copy-start | bytes 786436
  93.3 324.9 %copy-start.11 = (bf16[2,256,2,128]{3,1,2,0:T(8,128)(2,1)}, bf16[2,256,2,128]{3,1,2,0:T(8,128)(2,1)S(1)}, u32[]{:S(2)}) copy-start(bf16[2,256,2,128]{3,1,2,0:T(8,128)(2,1)S(1)} %all_gather.24) | copy-start | bytes 786436
  109.9 2.3 copy-start.18
  418.2 0.8 copy-start.13
  436.3 1.4 copy-start.14
  436.3 1.7 copy-start.15
  441.3 70.1 %reduce-scatter.3.cloned.1.call-start = ((), (), s32[]{:S(2)}) async-start(), calls=%async_computation.3 | async-start | bytes 327680 | tf_op jit(solution)/shard_map/reduce_scatter | solution.py:113
  459.5 164.6 %all-reduce.7.cloned.1.call-start = ((), (), s32[]{:S(2)}) async-start(), calls=%async_computation.4 | async-start | bytes 4194304 | tf_op jit(solution)/shard_map/psum | solution.py:136
  512.4 5.8 copy-start.8
  537.4 144.1 %all-gather.9.cloned.1.call-start = ((), (), s32[]{:S(2)}) async-start(), calls=%async_computation.5 | async-start | bytes 2621440 | tf_op jit(solution)/shard_map/all_gather | solution.py:51
  624.1 2.2 copy-start.6
  628.3 3.4 copy-start.3
  628.3 3.6 copy-start.4
  631.9 3.8 collective-permute-start
  635.6 0.8 copy-start.19
  636.5 61.6 %copy-start.12 = (bf16[2,256,2,128]{3,1,2,0:T(8,128)(2,1)S(1)}, bf16[2,256,2,128]{3,1,2,0:T(8,128)(2,1)}, u32[]{:S(2)}) copy-start(bf16[2,256,2,128]{3,1,2,0:T(8,128)(2,1)} %copy-done.11) | copy-start | bytes 786436
  636.5 125.5 %all-reduce.13.cloned.1.call-start = ((), (), s32[]{:S(2)}) async-start(), calls=%async_computation.11 | async-start | bytes 524288
  697.9 1.9 copy-start.16
  698.0 3.3 copy-start.21
  720.1 68.8 %reduce-scatter.5.cloned.1.call-start = ((), (), s32[]{:S(2)}) async-start(), calls=%async_computation.6 | async-start | bytes 327680 | tf_op jit(solution)/shard_map/reduce_scatter | solution.py:113
  738.3 163.4 %all-reduce.9.cloned.1.call-start = ((), (), s32[]{:S(2)}) async-start(), calls=%async_computation.7 | async-start | bytes 4194304 | tf_op jit(solution)/shard_map/psum | solution.py:136
  789.8 5.8 copy-start.7
  901.7 2.2 copy-start.5
  903.9 1.2 copy-start.10
  904.8 3.4 copy-start.1
Sparse Core Ops, SparseCore 0:
  8.9 48.6 all-gather.10
  59.2 44.7 all-gather.6
  105.8 295.8 all-gather.12
  441.4 43.0 all-reduce.10
  487.3 24.0 reduce-scatter.2
  537.5 86.5 all-reduce.6
  636.6 44.8 all-gather.8
  720.2 41.7 all-reduce.12
  764.8 24.0 reduce-scatter.4
  815.1 86.4 all-reduce.8
where the time goes:
time: 921 us; the launch traced here: 915 us
  waiting for transfers between devices  597 us (65%)
  matrix products  190 us (21%)
  local copies, waits for them, and re-layouts  62 us (7%)
  other arithmetic  29.4 us (3%)
  blocking collectives  20.2 us (2%)
  between operations  14.8 us (2%)
    all_gather x1, waiting for transfers between devices, on_device(): wo_layer = lax.all_gather(w_out[0], 'dp', axis=1, tiled=True)  286 us
    psum x2, waiting for transfers between devices, layer_grad(): lax.psum(partial_term.astype(jnp.bfloat16), 'tensor').astype(jnp.float32)  173 us
    unnamed x12, waiting for transfers between devices  49.9 us
    all_gather x2, waiting for transfers between devices, layer_grad(): lax.all_gather(own_upstream, 'tensor', axis=2, tiled=True)  44.8 us
    reduce_scatter x2, waiting for transfers between devices, layer_grad(): lax.psum_scatter(key_terms.astype(jnp.bfloat16), 'dp', scatter_dimension=...  40.6 us
    dot_general x1, local copies, waits for them, and re-layouts, layer_grad(): jnp.einsum('bpd,dc->bpc', normed, w_query, preferred_element_type=jnp.flo...  40 us
    dot_general x2, matrix products, layer_grad(): jnp.einsum('bpc,dc->bpd', grad_q, w_query, preferred_element_type=jnp.flo...  38.6 us
    dot_general x2, matrix products, layer_grad(): jnp.einsum('bpd,cd->bpc', g_whole, w_out, preferred_element_type=jnp.floa...  32.7 us
  transfers between devices with their start and end apart: 11, of which 9 were waited for; matrix products, arithmetic and copies ran while one was open for 15% of the time, Pallas kernels for 0%

commit v1 on v0

v1 whole, which is shorter than its diff:
```python
import functools
import math

import jax
import jax.numpy as jnp
from jax import lax
from jax.experimental import pallas as pl
from jax.experimental.pallas import tpu as pltpu
from jax.sharding import PartitionSpec as P

HD = 128
EPS = 1e-05
THETA = 500000.0
F32 = jnp.float32
BF16 = jnp.bfloat16


def dot_t(left, right):
    return lax.dot_general(left, right, (((1,), (1,)), ((), ())), preferred_element_type=F32)


def dot_n(left, right):
    return lax.dot_general(left, right, (((1,), (0,)), ((), ())), preferred_element_type=F32)


def dot_c(left, right):
    return lax.dot_general(left, right, (((0,), (0,)), ((), ())), preferred_element_type=F32)


def angle_tables(row_places):
    half_dim = HD // 2
    frequency = THETA ** (-(jnp.arange(half_dim, dtype=F32) * 2.0) / HD)
    angles = row_places[:, None] * frequency[None, :]
    cosine = jnp.concatenate([jnp.cos(angles), jnp.cos(angles)], -1)
    signed_sine = jnp.concatenate([-jnp.sin(angles), jnp.sin(angles)], -1)
    return cosine, signed_sine


def turn_plain(values):
    half_dim = HD // 2
    return jnp.concatenate([values[..., half_dim:], values[..., :half_dim]], -1)


def attention_body(lens_ref, q_ref, o_ref, k_ref, v_ref, cos_ref, sin_ref, gq_ref, gk_ref, gv_ref):
    seq = pl.program_id(0)
    rows = q_ref.shape[1]
    length = k_ref.shape[1]
    group = q_ref.shape[2] // HD
    scale = 1.0 / math.sqrt(HD)
    cosine, sine = cos_ref[...], sin_ref[...]
    q_parts, o_parts = [], []
    for head in range(group):
        lanes = slice(head * HD, (head + 1) * HD)
        raw = q_ref[0, :, lanes]
        q_parts.append((raw * cosine + pltpu.roll(raw, HD // 2, 1) * sine).astype(BF16))
        o_parts.append(o_ref[0, :, lanes])
    q_all = jnp.concatenate(q_parts, 0)
    o_all = jnp.concatenate(o_parts, 0)
    keys, values = k_ref[0], v_ref[0]
    many = rows * group
    row_at = lax.broadcasted_iota(jnp.int32, (many, length), 0) & (rows - 1)
    query_at = lens_ref[1, 0] + row_at
    key_at = lax.broadcasted_iota(jnp.int32, (many, length), 1)
    start = length - lens_ref[0, seq]
    allowed = (key_at == query_at) | ((key_at < query_at) & (key_at >= start))
    scores = jnp.where(allowed, dot_t(q_all, keys) * scale, -1e30)
    highest = jnp.max(scores, -1, keepdims=True)
    terms = jnp.where(allowed, jnp.exp(scores - highest), 0.0)
    probs = terms / jnp.sum(terms, -1, keepdims=True)
    grad_probs = dot_t(o_all, values)
    row_dot = jnp.sum(probs * grad_probs, -1, keepdims=True)
    grad_scores = (probs * (grad_probs - row_dot) * scale).astype(BF16)
    grad_qr = dot_n(grad_scores, keys)
    gk_ref[0] = dot_c(grad_scores, q_all).astype(BF16)
    gv_ref[0] = dot_c(probs.astype(BF16), o_all).astype(BF16)
    for head in range(group):
        part = grad_qr[head * rows : (head + 1) * rows]
        turned = part * cosine - pltpu.roll(part, HD // 2, 1) * sine
        gq_ref[0, :, head * HD : (head + 1) * HD] = turned.astype(BF16)


def attention_grad(lens, queries, grad_out, keys, values, cosine, sine):
    batch, rows, cols = queries.shape
    length = keys.shape[1]
    kv_dev = keys.shape[2] // HD
    group_cols = cols // kv_dev
    q_spec = pl.BlockSpec((1, rows, group_cols), lambda b, h: (b, 0, h))
    k_spec = pl.BlockSpec((1, length, HD), lambda b, h: (b, 0, h))
    t_spec = pl.BlockSpec((rows, HD), lambda b, h: (0, 0))
    return pl.pallas_call(
        attention_body,
        grid=(batch, kv_dev),
        in_specs=[
            pl.BlockSpec(memory_space=pltpu.SMEM),
            q_spec,
            q_spec,
            k_spec,
            k_spec,
            t_spec,
            t_spec,
        ],
        out_specs=[q_spec, k_spec, k_spec],
        out_shape=[
            jax.ShapeDtypeStruct((batch, rows, cols), BF16),
            jax.ShapeDtypeStruct((batch, length, kv_dev * HD), BF16),
            jax.ShapeDtypeStruct((batch, length, kv_dev * HD), BF16),
        ],
        compiler_params=pltpu.CompilerParams(vmem_limit_bytes=32 * 1024 * 1024),
    )(lens, queries, grad_out, keys, values, cosine, sine)


def on_device(
    n_dp, n_tensor, stored, cotangent, positions, lengths, norm_gain, w_query, w_key, w_value, w_out
):
    x_own = stored[0]
    gain = norm_gain[0]
    w_q, w_k, w_v, w_o = w_query[0], w_key[0], w_value[0], w_out[0]
    seqs, rows, width_dev = x_own.shape
    many = seqs * rows
    width = gain.shape[0]
    kv_cols = w_k.shape[1]
    dp_id = lax.axis_index("dp")
    tensor_id = lax.axis_index("tensor")
    section_id = lax.axis_index("section")
    swap = [(d * n_tensor + t, t * n_tensor + d) for d in range(n_dp) for t in range(n_tensor)]

    row_ids = dp_id * rows + jnp.arange(rows, dtype=jnp.int32)
    cosine, sine = angle_tables(row_ids.astype(F32))
    lens = jnp.stack(
        [lengths, jnp.full_like(lengths, dp_id * rows)], 0
    )

    cot_slice = lax.ppermute(cotangent, ("dp", "tensor"), swap)
    resp = cotangent.shape[1]
    resp_part = dot_t(cot_slice.reshape(seqs * resp, width_dev), w_o)
    resp_grad = lax.psum(resp_part.astype(BF16), "dp").reshape(seqs, resp, -1)
    placed = (positions[:, None, :] == row_ids[None, :, None]).astype(BF16)

    def place(small):
        return jnp.einsum("spr,srd->spd", placed, small, preferred_element_type=F32).astype(BF16)

    x_whole = lax.all_gather(x_own, "tensor", axis=2, tiled=True)
    x_full = x_whole.astype(F32)
    inv_rms = lax.rsqrt(jnp.mean(x_full * x_full, -1, keepdims=True) + EPS)
    normed = (x_full * inv_rms * gain).astype(BF16).reshape(many, width)
    queries, keys, values = lax.optimization_barrier(
        (dot_n(normed, w_q), dot_n(normed, w_k), dot_n(normed, w_v))
    )
    k_four = keys.reshape(seqs, rows, -1, HD)
    k_rot = k_four * cosine[:, None] + turn_plain(k_four) * sine[:, None]
    kv_own = jnp.concatenate(
        [k_rot.reshape(seqs, rows, kv_cols), values.reshape(seqs, rows, kv_cols)], -1
    ).astype(BF16)
    kv_all = lax.all_gather(kv_own, "dp", axis=1, tiled=True)
    k_all, v_all = kv_all[..., :kv_cols], kv_all[..., kv_cols:]
    queries = queries.reshape(seqs, rows, -1)
    gain_own = lax.dynamic_slice_in_dim(gain, tensor_id * width_dev, width_dev, 0)
    x_mine = x_own.astype(F32)

    def backward(upstream_own, grad_out):
        grad_q, key_terms, value_terms = attention_grad(
            lens, queries, grad_out, k_all, v_all, cosine, sine
        )
        kv_sum = lax.psum_scatter(
            jnp.concatenate([key_terms, value_terms], -1), "dp", scatter_dimension=1, tiled=True
        ).astype(F32)
        gk_four = kv_sum[..., :kv_cols].reshape(seqs, rows, -1, HD)
        grad_k = gk_four * cosine[:, None] - turn_plain(gk_four) * sine[:, None]
        grad_k = grad_k.astype(BF16).reshape(many, kv_cols)
        grad_v = kv_sum[..., kv_cols:].astype(BF16).reshape(many, kv_cols)
        partial = dot_t(grad_q.reshape(many, -1), w_q) + dot_t(grad_k, w_k) + dot_t(grad_v, w_v)
        summed = lax.psum_scatter(
            partial.astype(BF16), "tensor", scatter_dimension=1, tiled=True
        ).astype(F32)
        summed = summed.reshape(seqs, rows, width_dev)
        stat = lax.psum(jnp.sum(x_mine * gain_own * summed, -1, keepdims=True), "tensor")
        return (
            upstream_own.astype(F32)
            + inv_rms * gain_own * summed
            - x_mine * inv_rms**3 * stat / width
        )

    first = backward(place(cotangent), place(resp_grad))

    first_b = first.astype(BF16)
    down = [(1, 0)]
    handed = lax.ppermute(first_b, "section", down)
    across = [
        ((d * 2 + 1) * n_tensor + t, (t * 2) * n_tensor + d)
        for d in range(n_dp)
        for t in range(n_tensor)
    ]
    crossed = lax.ppermute(first_b, ("dp", "section", "tensor"), across)
    up_rows = lax.all_gather(crossed, "tensor", axis=0, tiled=False)
    up_part = dot_t(up_rows.reshape(n_dp * many, width_dev), w_o).astype(BF16)
    grad_out = lax.psum_scatter(up_part, "dp", scatter_dimension=0, tiled=True)
    second = backward(handed, grad_out.reshape(seqs, rows, -1))
    return jnp.where(section_id == 0, second, first)[None]


def solution(mesh):
    return jax.shard_map(
        functools.partial(on_device, mesh.shape["dp"], mesh.shape["tensor"]),
        mesh=mesh,
        in_specs=(
            P("section", None, "dp", "tensor"),
            P(None, None, "tensor"),
            P(),
            P(),
            P("section", None),
            P("section", None, "tensor"),
            P("section", None, "tensor"),
            P("section", None, "tensor"),
            P("section", "tensor", "dp"),
        ),
        out_specs=P("section", None, "dp", "tensor"),
        check_vma=False,
    )
```

time: 921 us -> 432 us (0.47)
  waiting for transfers between devices: 597 us -> 264 us
  matrix products: 190 us -> 86 us
  local copies, waits for them, and re-layouts: 62 us -> 4.76 us
  other arithmetic: 29.4 us -> 15.6 us
  blocking collectives: 20.2 us -> 30.2 us
  Pallas kernels: 0 us -> 9.74 us
    all_gather x4 -> x2, waiting for transfers between devices: 330 us -> 64.7 us  [the longest x1 61.5 us: on_device(): up_rows = lax.all_gather(crossed, 'tensor', axis=0, tiled=False)]
    psum x2 -> x1, waiting for transfers between devices: 173 us -> 64.5 us  [on_device(): resp_grad = lax.psum(resp_part.astype(BF16), 'dp').reshape(seqs, resp, -1)]
    dot_general x20 -> x13, matrix products: 188 us -> 86 us  [the longest x8 67.6 us: dot_t(): lax.dot_general(left, right, (((1,), (1,)), ((), ())), preferred_element_...]
    reduce_scatter x2 -> x5, waiting for transfers between devices: 40.6 us -> 132 us  [the longest x2 85.8 us: backward(): lax.psum_scatter(partial.astype(BF16), 'tensor', scatter_dimension=1, til...]
    dot_general x3 -> x0, local copies, waits for them, and re-layouts: 52.9 us -> none  [the longest x1 40 us: layer_grad(): jnp.einsum('bpd,dc->bpc', normed, w_query, preferred_element_type=jnp.flo...]
    unnamed x12 -> x8, waiting for transfers between devices: 49.9 us -> 0.64 us
    psum x0 -> x2, blocking collectives: none -> 20.2 us  [backward(): lax.psum(jnp.sum(x_mine * gain_own * summed, -1, keepdims=True), 'tensor')]
    all_gather x2 -> x1, blocking collectives: 20.2 us -> 10 us  [on_device(): kv_all = lax.all_gather(kv_own, 'dp', axis=1, tiled=True)]
  transfers between devices with their start and end apart: 11 -> 11, of which waited for: 9 -> 9; matrix products, arithmetic and copies ran while one was open for 15% -> 9% of each run, Pallas kernels for 0% -> 0%
where the time goes in v1:
time: 432 us; the launch traced here: 431 us
  waiting for transfers between devices  264 us (61%)
  matrix products  86 us (20%)
  blocking collectives  30.2 us (7%)
  other arithmetic  15.6 us (4%)
  between operations  15.2 us (4%)
  Pallas kernels  9.74 us (2%)
  starting transfers between devices  4.87 us (1%)
  local copies, waits for them, and re-layouts  4.76 us (1%)
    reduce_scatter x2, waiting for transfers between devices, backward(): lax.psum_scatter(partial.astype(BF16), 'tensor', scatter_dimension=1, til...  85.8 us
    dot_general x8, matrix products, dot_t(): lax.dot_general(left, right, (((1,), (1,)), ((), ())), preferred_element_...  67.6 us
    psum x1, waiting for transfers between devices, on_device(): resp_grad = lax.psum(resp_part.astype(BF16), 'dp').reshape(seqs, resp, -1)  64.5 us
    all_gather x1, waiting for transfers between devices, on_device(): up_rows = lax.all_gather(crossed, 'tensor', axis=0, tiled=False)  61.5 us
    reduce_scatter x1, waiting for transfers between devices, on_device(): grad_out = lax.psum_scatter(up_part, 'dp', scatter_dimension=0, tiled=True)  34.1 us
    psum x2, blocking collectives, backward(): lax.psum(jnp.sum(x_mine * gain_own * summed, -1, keepdims=True), 'tensor')  20.2 us
    dot_general x3, matrix products, dot_n(): lax.dot_general(left, right, (((1,), (0,)), ((), ())), preferred_element_...  14.5 us
    reduce_scatter x2, waiting for transfers between devices, backward(): lax.psum_scatter(jnp.concatenate([key_terms, value_terms], -1), 'dp', sca...  12.2 us
  transfers between devices with their start and end apart: 11, of which 9 were waited for; matrix products, arithmetic and copies ran while one was open for 9% of the time, Pallas kernels for 0%

profile of v1, /device:TPU:0, one launch (start us, length us, event | category | flops | bytes accessed | tf_op | source)
XLA Modules:
  0.0 430.8 jit_solution(1050594760607525504)
XLA Ops:
  7.4 1.6 collective-permute-start
  9.0 6.8 %fusion.29 = bf16[64,2048]{1,0:T(8,128)(2,1)} fusion(bf16[64,2048]{1,0:T(8,128)(2,1)S(1)} %bitcast.113, bf16[1,2048,2048]{2,1,0:T(8,128)(2,1)} %param.17), kind=kOutput, calls=%fused_computation.35 | convolution fusion | flops 537001984 | bytes 8912896 | tf_op jit(solution)/shard_map/dot_general | solution.py:19
  15.8 0.5 all-gather.5.cloned.1.call-update
  16.4 0.2 multiply_cosine_fusion
  16.6 0.1 pad_maximum_fusion.6
  16.9 64.5 %all-reduce.3.cloned.1.call-done = bf16[2,32,2048]{2,1,0:T(8,128)(2,1)} async-done(((bf16[2,32,2048]{2,1,0:T(8,128)(2,1)}), bf16[2,32,2048]{2,1,0:T(8,128)(2,1)}) %all-reduce.3.cloned.1.call-update) | async-done | bytes 262160 | tf_op jit(solution)/shard_map/psum | solution.py:136
  81.3 1.4 convolution_convert_fusion.o_ref
  82.7 3.2 all-gather.5.cloned.1.call-done
  85.8 2.1 fusion.12
  88.0 2.2 fusion.14
  90.2 13.1 %fusion.4 = f32[128,2048]{1,0:T(8,128)S(1)} fusion(bf16[128,8192]{1,0:T(8,128)(2,1)S(1)} %bitcast.95, bf16[1,8192,2048]{2,1,0:T(8,128)(2,1)} %param.14), kind=kOutput, calls=%fused_computation.4 | convolution fusion | flops 4294967296 | bytes 36700160 | tf_op jit(solution)/shard_map/dot_general | solution.py:23
  103.2 0.7 fusion.21
  104.0 1.5 copy-done.2
  105.4 0.7 fusion.17
  106.1 0.1 reshape.128
  106.2 0.2 fusion.49
  106.4 0.2 pad_maximum_fusion.2
  106.6 0.1 concatenate.33
  106.8 10.0 %all_gather.13 = bf16[2,256,512]{2,1,0:T(8,128)(2,1)S(1)} all-gather(bf16[2,64,512]{2,1,0:T(8,128)(2,1)S(1)} %pad_maximum_fusion.3), channel_id=1, replica_groups=mesh['dp'=4,'section'=2,'tensor'=4] {'dp'}, dimensions={1}, use_global_device_ids=true | all-gather | bytes 655360 | tf_op jit(solution)/shard_map/all_gather | solution.py:154
  116.8 4.9 %shard_map.91 = (bf16[2,64,2048]{2,1,0:T(8,128)(2,1)S(1)}, bf16[2,256,256]{2,1,0:T(8,128)(2,1)S(1)}, bf16[2,256,256]{2,1,0:T(8,128)(2,1)S(1)}) custom-call(s32[2,2]{1,0:T(2,128)S(1)} %stack.7.lens_ref, f32[2,64,2048]{2,1,0:T(8,128)S(1)} %bitcast.90, bf16[2,64,2048]{2,1,0:T(8,128)(2,1)S(1)} %convolution_convert_fusion.o_ref, ...), custom_call_target="tpu_custom_call" | custom-call | tf_op jit(solution)/shard_map/pallas_call | solution.py:90
  121.7 0.8 pad_maximum_fusion
  122.6 0.2 reduce-scatter.8.cloned.1.call-start
  122.8 17.5 %fusion.2 = f32[128,8192]{1,0:T(8,128)} fusion(bf16[128,2048]{1,0:T(8,128)(2,1)S(1)} %bitcast.93, bf16[1,8192,2048]{2,1,0:T(8,128)(2,1)} %param.14), kind=kOutput, calls=%fused_computation.2 | convolution fusion | flops 4294967296 | bytes 38273024 | tf_op jit(solution)/shard_map/dot_general | solution.py:19
  140.3 5.1 %reduce-scatter.6.cloned.1.call-done = bf16[2,64,512]{2,1,0:T(8,128)(2,1)} async-done(((bf16[2,256,512]{2,1,0:T(8,128)(2,1)}), bf16[2,64,512]{2,1,0:T(8,128)(2,1)}) %reduce-scatter.6.cloned.1.call-update) | async-done | bytes 131088 | tf_op jit(solution)/shard_map/reduce_scatter | solution.py:164
  145.4 0.9 fusion.47
  146.3 0.1 reshape.131
  146.4 0.2 fusion.48
  146.6 0.2 pad_maximum_fusion.4
  146.8 0.1 concatenate.38
  146.9 0.9 subtract_convert_fusion.1
  147.8 5.1 %convolution_add_fusion.3 = f32[128,8192]{1,0:T(8,128)S(1)} fusion(f32[128,8192]{1,0:T(8,128)} %fusion.2, bf16[128,256]{1,0:T(8,128)(2,1)S(1)} %bitcast.112, bf16[1,8192,256]{2,1,0:T(8,128)(2,1)} %param.15), kind=kOutput, calls=%fused_computation.9 | convolution fusion | flops 537919488 | bytes 12648448 | tf_op jit(solution)/shard_map/dot_general | solution.py:19
  152.9 2.9 fusion.6
  155.8 0.0 all-gather.7.cloned.1.call-start
  155.9 43.5 %reduce-scatter.8.cloned.1.call-done = bf16[128,2048]{1,0:T(8,128)(2,1)} async-done(((bf16[128,8192]{1,0:T(8,128)(2,1)}), bf16[128,2048]{1,0:T(8,128)(2,1)}) %reduce-scatter.8.cloned.1.call-update) | async-done | bytes 524304 | tf_op jit(solution)/shard_map/reduce_scatter | solution.py:172
  199.4 1.3 multiply_reduce_fusion.1
  200.7 0.1 mul.224
  200.8 10.1 %psum.22 = f32[2,64]{1,0:T(2,128)S(1)} all-reduce(f32[2,64]{1,0:T(2,128)S(1)} %mul.224), channel_id=1, replica_groups=mesh['dp'=4,'section'=2,'tensor'=4] {'tensor'}, use_global_device_ids=true, to_apply=%region_5.0 | all-reduce | flops 128 | bytes 1024 | tf_op jit(solution)/shard_map/psum | solution.py:176
  210.9 2.6 fusion.50
  213.5 1.3 collective-permute-start.2
  214.7 2.5 collective-permute-done.2
  217.2 0.8 copy-done.7
  218.1 61.5 %all-gather.7.cloned.1.call-done = bf16[8,64,2048]{2,1,0:T(8,128)(2,1)} async-done(((bf16[2,64,2048]{2,1,0:T(8,128)(2,1)}), bf16[8,64,2048]{2,1,0:T(8,128)(2,1)}) %all-gather.7.cloned.1.call-update) | async-done | bytes 2097168 | tf_op jit(solution)/shard_map/all_gather | solution.py:194
  279.6 9.9 %fusion.23 = bf16[512,2048]{1,0:T(8,128)(2,1)} fusion(bf16[512,2048]{1,0:T(8,128)(2,1)} %bitcast.122, bf16[1,2048,2048]{2,1,0:T(8,128)(2,1)} %param.17), kind=kOutput, calls=%fused_computation.29 | convolution fusion | flops 4296015872 | bytes 12582912 | tf_op jit(solution)/shard_map/dot_general | solution.py:19
  289.6 34.1 %reduce-scatter.10.cloned.1.call-done = bf16[128,2048]{1,0:T(8,128)(2,1)} async-done(((bf16[512,2048]{1,0:T(8,128)(2,1)}), bf16[128,2048]{1,0:T(8,128)(2,1)}) %reduce-scatter.10.cloned.1.call-update) | async-done | bytes 524304 | tf_op jit(solution)/shard_map/reduce_scatter | solution.py:196
  323.7 1.0 copy-done
  324.8 4.9 %shard_map.92 = (bf16[2,64,2048]{2,1,0:T(8,128)(2,1)S(1)}, bf16[2,256,256]{2,1,0:T(8,128)(2,1)S(1)}, bf16[2,256,256]{2,1,0:T(8,128)(2,1)S(1)}) custom-call(s32[2,2]{1,0:T(2,128)S(1)} %stack.7.lens_ref, f32[2,64,2048]{2,1,0:T(8,128)S(1)} %bitcast.91, bf16[2,64,2048]{2,1,0:T(8,128)(2,1)S(1)} %bitcast.94, bf16[2,256,256]{2,1,0:T(8,128)(2,1)S(1)} %get-tuple-element.24.k_ref, ...), custom_call_target="tpu_custom_call" | custom-call | tf_op jit(solution)/shard_map/pallas_call | solution.py:90
  329.6 0.8 pad_maximum_fusion.1
  330.5 0.3 reduce-scatter.14.cloned.1.call-start
  330.8 17.5 %fusion = f32[128,8192]{1,0:T(8,128)} fusion(bf16[128,2048]{1,0:T(8,128)(2,1)S(1)} %bitcast.92, bf16[1,8192,2048]{2,1,0:T(8,128)(2,1)} %param.14), kind=kOutput, calls=%fused_computation | convolution fusion | flops 4294967296 | bytes 38273024 | tf_op jit(solution)/shard_map/dot_general | solution.py:19
  348.3 7.1 %reduce-scatter.12.cloned.1.call-done = bf16[2,64,512]{2,1,0:T(8,128)(2,1)} async-done(((bf16[2,256,512]{2,1,0:T(8,128)(2,1)}), bf16[2,64,512]{2,1,0:T(8,128)(2,1)}) %reduce-scatter.12.cloned.1.call-update) | async-done | bytes 131088 | tf_op jit(solution)/shard_map/reduce_scatter | solution.py:164
  355.4 0.9 fusion.45
  356.3 0.1 reshape.137
  356.4 0.2 fusion.46
  356.6 0.2 pad_maximum_fusion.5
  356.8 0.1 concatenate.41
  356.9 0.9 subtract_convert_fusion
  357.8 5.1 %convolution_add_fusion.1 = f32[128,8192]{1,0:T(8,128)S(1)} fusion(f32[128,8192]{1,0:T(8,128)} %fusion, bf16[128,256]{1,0:T(8,128)(2,1)S(1)} %bitcast.111, bf16[1,8192,256]{2,1,0:T(8,128)(2,1)} %param.15), kind=kOutput, calls=%fused_computation.7 | convolution fusion | flops 537919488 | bytes 12648448 | tf_op jit(solution)/shard_map/dot_general | solution.py:19
  362.9 2.9 fusion.7
  365.8 1.3 collective-permute-start.1
  367.1 42.3 %reduce-scatter.14.cloned.1.call-done = bf16[128,2048]{1,0:T(8,128)(2,1)} async-done(((bf16[128,8192]{1,0:T(8,128)(2,1)}), bf16[128,2048]{1,0:T(8,128)(2,1)}) %reduce-scatter.14.cloned.1.call-update) | async-done | bytes 524304 | tf_op jit(solution)/shard_map/reduce_scatter | solution.py:172
  409.4 1.3 multiply_reduce_fusion
  410.7 0.1 mul.231
  410.8 10.1 %psum.23 = f32[2,64]{1,0:T(2,128)S(1)} all-reduce(f32[2,64]{1,0:T(2,128)S(1)} %mul.231), channel_id=1, replica_groups=mesh['dp'=4,'section'=2,'tensor'=4] {'tensor'}, use_global_device_ids=true, to_apply=%region_10.0 | all-reduce | flops 128 | bytes 1024 | tf_op jit(solution)/shard_map/psum | solution.py:176
  420.9 2.5 fusion.35
  (48 shorter events, 0.5 us)
Async XLA Ops:
  7.4 73.9 %all-reduce.3.cloned.1.call-start = ((), (), s32[]{:S(2)}) async-start(), calls=%async_computation.5 | async-start | bytes 524288 | tf_op jit(solution)/shard_map/psum | solution.py:136
  7.4 1.6 collective-permute-start
  9.0 7.8 %copy-start.11 = (s32[2]{0:T(128)S(1)}, s32[2]{0:T(128)}, u32[]{:S(2)}) copy-start(s32[2]{0:T(128)} %param.12) | copy-start | bytes 28
  9.0 72.3 %copy-start.10 = (s32[2,32]{1,0:T(2,128)S(1)}, s32[2,32]{1,0:T(2,128)}, u32[]{:S(2)}) copy-start(s32[2,32]{1,0:T(2,128)} %param.11) | copy-start | bytes 772
  15.7 72.2 %copy-start.9 = (f32[1,8192]{1,0:T(1,128)S(1)}, f32[1,8192]{1,0:T(1,128)}, u32[]{:S(2)}) copy-start(f32[1,8192]{1,0:T(1,128)} %param.13) | copy-start | bytes 98308
  15.8 70.1 %all-gather.5.cloned.1.call-start = ((), (), s32[]{:S(2)}) async-start(), calls=%async_computation.11 | async-start | bytes 2621440 | tf_op jit(solution)/shard_map/all_gather | solution.py:142
  16.3 129.0 %reduce-scatter.6.cloned.1.call-start = ((), (), s32[]{:S(2)}) async-start(), calls=%async_computation.6 | async-start | bytes 655360 | tf_op jit(solution)/shard_map/reduce_scatter | solution.py:164
  90.1 13.1 %copy-start.1 = (bf16[1,8192,256]{2,1,0:T(8,128)(2,1)S(1)}, bf16[1,8192,256]{2,1,0:T(8,128)(2,1)}, u32[]{:S(2)}) copy-start(bf16[1,8192,256]{2,1,0:T(8,128)(2,1)} %param.15) | copy-start | bytes 12582916
  103.2 2.2 copy-start.2
  122.6 76.8 %reduce-scatter.8.cloned.1.call-start = ((), (), s32[]{:S(2)}) async-start(), calls=%async_computation.7 | async-start | bytes 2621440 | tf_op jit(solution)/shard_map/reduce_scatter | solution.py:172
  147.8 5.1 %copy-start.3 = (bf16[1,8192,256]{2,1,0:T(8,128)(2,1)S(1)}, bf16[1,8192,256]{2,1,0:T(8,128)(2,1)}, u32[]{:S(2)}) copy-start(bf16[1,8192,256]{2,1,0:T(8,128)(2,1)} %param.16) | copy-start | bytes 12582916
  152.9 46.5 %copy-start.5 = (bf16[1,2,64,2048]{3,2,1,0:T(8,128)(2,1)S(1)}, bf16[1,2,64,2048]{3,2,1,0:T(8,128)(2,1)}, u32[]{:S(2)}) copy-start(bf16[1,2,64,2048]{3,2,1,0:T(8,128)(2,1)} %param.9) | copy-start | bytes 1572868
  152.9 58.0 %copy-start.8 = (bf16[2,32,2048]{2,1,0:T(8,128)(2,1)S(1)}, bf16[2,32,2048]{2,1,0:T(8,128)(2,1)}, u32[]{:S(2)}) copy-start(bf16[2,32,2048]{2,1,0:T(8,128)(2,1)} %param.10) | copy-start | bytes 786436
  155.8 123.8 %all-gather.7.cloned.1.call-start = ((), (), s32[]{:S(2)}) async-start(), calls=%async_computation.12 | async-start | bytes 2621440 | tf_op jit(solution)/shard_map/all_gather | solution.py:194
  213.5 3.8 collective-permute-start.2
  217.2 0.8 copy-start.7
  218.1 105.6 %reduce-scatter.10.cloned.1.call-start = ((), (), s32[]{:S(2)}) async-start(), calls=%async_computation.8 | async-start | bytes 2621440 | tf_op jit(solution)/shard_map/reduce_scatter | solution.py:196
  289.5 65.9 %reduce-scatter.12.cloned.1.call-start = ((), (), s32[]{:S(2)}) async-start(), calls=%async_computation.9 | async-start | bytes 655360 | tf_op jit(solution)/shard_map/reduce_scatter | solution.py:164
  323.7 1.0 copy-start
  330.5 78.9 %reduce-scatter.14.cloned.1.call-start = ((), (), s32[]{:S(2)}) async-start(), calls=%async_computation.10 | async-start | bytes 2621440 | tf_op jit(solution)/shard_map/reduce_scatter | solution.py:172
  357.8 5.1 %copy-start.4 = (bf16[1,8192,256]{2,1,0:T(8,128)(2,1)S(1)}, bf16[1,8192,256]{2,1,0:T(8,128)(2,1)}, u32[]{:S(2)}) copy-start(bf16[1,8192,256]{2,1,0:T(8,128)(2,1)} %param.16) | copy-start | bytes 12582916
  362.9 58.0 %copy-start.6 = (f32[2,64,2048]{2,1,0:T(8,128)S(1)}, f32[2,64,2048]{2,1,0:T(8,128)}, u32[]{:S(2)}) copy-start(f32[2,64,2048]{2,1,0:T(8,128)} %get-tuple-element.41) | copy-start | bytes 3145732
  365.8 55.1 %collective-permute-start.1 = (bf16[2,64,2048]{2,1,0:T(8,128)(2,1)S(1)}, bf16[2,64,2048]{2,1,0:T(8,128)(2,1)S(1)}, u32[]{:S(2)}, u32[]{:S(2)}) collective-permute-start(bf16[2,64,2048]{2,1,0:T(8,128)(2,1)S(1)} %get-tuple-element.40), channel_id=1, source_target_pairs={{4,0},{5,1},{6,2},{7,3},{12,8},{13,9},{14,10},{15,11},{20,16},{21,... | collective-permute-start | bytes 1572872 | tf_op jit(solution)/shard_map/ppermute | solution.py:187
Sparse Core Ops, SparseCore 0:
  15.9 65.3 all-reduce.2
  122.7 22.6 reduce-scatter.5
  289.7 34.0 reduce-scatter.9
  330.6 24.7 reduce-scatter.11
Sparse Core Ops, SparseCore 1:
  17.8 68.0 all-gather.4
  155.9 43.4 reduce-scatter.7
  218.2 61.4 all-gather.6
  365.9 43.4 reduce-scatter.13

commit v2 on v1

--- a/solution.py
+++ b/solution.py
@@ -109,8 +109,442 @@
     )(lens, queries, grad_out, keys, values, cosine, sine)
 
 
+MESH = pl.DeviceIdType.MESH
+BIG = 56 * 1024 * 1024
+
+
+def at(dp, section, tensor):
+    return {"dp": dp, "section": section, "tensor": tensor}
+
+
+def greet(where):
+    pl.semaphore_signal(
+        pltpu.get_barrier_semaphore(), inc=1, device_id=where, device_id_type=MESH
+    )
+
+
+def remote(src, dst, send_sem, recv_sem, where):
+    return pltpu.make_async_remote_copy(
+        src_ref=src,
+        dst_ref=dst,
+        send_sem=send_sem,
+        recv_sem=recv_sem,
+        device_id=where,
+        device_id_type=MESH,
+    )
+
+
+def tiled_dot_t(left_ref, w_ref, store):
+    tile = 256
+    left = left_ref[...]
+
+    def step(index, carry):
+        start = pl.multiple_of(index * tile, tile)
+        store(start, tile, dot_t(left, w_ref[pl.ds(start, tile), :]).astype(BF16))
+        return carry
+
+    lax.fori_loop(0, w_ref.shape[0] // tile, step, 0)
+
+
+def opening_body(
+    n, x_ref, cot_ref, w_ref, x_out, resp_out, cot_in, w_in, part, inbox,
+    x_send, x_recv, cot_sems, w_sem, part_send, part_recv, own_sem, turn_sem,
+):
+    d, sec, t = lax.axis_index("dp"), lax.axis_index("section"), lax.axis_index("tensor")
+    crossing = jnp.where(d == t, 0, 1)
+    for k in range(1, n):
+        greet(at(d, sec, lax.rem(t + k, n)))
+        greet(at(lax.rem(d + k, n), sec, t))
+    greet(at(d, 1 - sec, t))
+
+    @pl.when(d != t)
+    def _():
+        greet(at(t, sec, d))
+
+    pl.semaphore_wait(pltpu.get_barrier_semaphore(), 2 * n - 1 + crossing)
+
+    own = pltpu.make_async_copy(x_ref, x_out.at[t], own_sem)
+    own.start()
+
+    @pl.when(sec == 0)
+    def _():
+        pl.semaphore_wait(turn_sem, 1)
+
+    def pass_on(src, slot, right):
+        step = 1 if right else -1
+        return remote(
+            src, x_out.at[slot], x_send.at[slot, int(right)], x_recv.at[slot],
+            at(d, sec, t + step),
+        )
+
+    @pl.when(t + 1 < n)
+    def _():
+        pass_on(x_ref, t, True).start()
+
+    @pl.when(t > 0)
+    def _():
+        pass_on(x_ref, t, False).start()
+
+    @pl.when(sec == 1)
+    def _():
+        load = pltpu.make_async_copy(w_ref, w_in, w_sem)
+        load.start()
+        swap = remote(cot_ref, cot_in, cot_sems.at[0], cot_sems.at[1], at(t, sec, d))
+        keep = pltpu.make_async_copy(cot_ref, cot_in, cot_sems.at[2])
+
+        @pl.when(d != t)
+        def _():
+            swap.start()
+            swap.wait()
+
+        @pl.when(d == t)
+        def _():
+            keep.start()
+            keep.wait()
+
+        load.wait()
+
+        def store(start, size, value):
+            part[:, pl.ds(start, size)] = value
+
+        tiled_dot_t(cot_in, w_in, store)
+        for k in range(1, n):
+            remote(
+                part, inbox.at[d], part_send.at[k], part_recv.at[d],
+                at(lax.rem(d + k, n), sec, t),
+            ).start()
+
+    for k in range(1, n):
+        left, right = t - k, t + k
+
+        @pl.when(left >= 0)
+        def _():
+            pass_on(x_ref, left, True).wait_recv()
+
+            @pl.when(t + 1 < n)
+            def _():
+                pass_on(x_out.at[left], left, True).start()
+
+        @pl.when(right < n)
+        def _():
+            pass_on(x_ref, right, False).wait_recv()
+
+            @pl.when(t > 0)
+            def _():
+                pass_on(x_out.at[right], right, False).start()
+
+    own.wait()
+
+    @pl.when(sec == 1)
+    def _():
+        pl.semaphore_signal(turn_sem, inc=1, device_id=at(d, 0, t), device_id_type=MESH)
+        total = part[...].astype(F32)
+        for k in range(1, n):
+            peer = lax.rem(d + k, n)
+            move = remote(
+                part, inbox.at[peer], part_send.at[k], part_recv.at[peer], at(peer, sec, t)
+            )
+            move.wait_recv()
+            total = total + inbox[peer].astype(F32)
+        resp_out[...] = total.astype(BF16)
+        for k in range(1, n):
+            peer = lax.rem(d + k, n)
+            remote(
+                part, inbox.at[d], part_send.at[k], part_recv.at[d], at(peer, sec, t)
+            ).wait_send()
+
+    for k in range(n):
+        left, right = t - k, t + k
+
+        @pl.when((left >= 0) & (t + 1 < n))
+        def _():
+            pass_on(x_ref, left, True).wait_send()
+
+        @pl.when((right < n) & (t > 0))
+        def _():
+            pass_on(x_ref, right, False).wait_send()
+
+
+def opening(n, x, cot, w):
+    many, wide = x.shape
+    resp = cot.shape[0]
+    cols = w.shape[0]
+    dma = pltpu.SemaphoreType.DMA
+    return pl.pallas_call(
+        functools.partial(opening_body, n),
+        in_specs=[pl.BlockSpec(memory_space=pl.ANY)] * 3,
+        out_specs=[
+            pl.BlockSpec(memory_space=pl.ANY),
+            pl.BlockSpec(memory_space=pltpu.VMEM),
+        ],
+        out_shape=[
+            jax.ShapeDtypeStruct((n, many, wide), BF16),
+            jax.ShapeDtypeStruct((resp, cols), BF16),
+        ],
+        scratch_shapes=[
+            pltpu.VMEM((resp, wide), BF16),
+            pltpu.VMEM(w.shape, BF16),
+            pltpu.VMEM((resp, cols), BF16),
+            pltpu.VMEM((n, resp, cols), BF16),
+            dma((n, 2)),
+            dma((n,)),
+            dma((3,)),
+            dma,
+            dma((n,)),
+            dma((n,)),
+            dma,
+            pltpu.SemaphoreType.REGULAR,
+        ],
+        compiler_params=pltpu.CompilerParams(
+            collective_id=0, has_side_effects=True, vmem_limit_bytes=BIG
+        ),
+    )(x, cot, w)
+
+
+def finish_body(
+    n, active, width, part_ref, x_ref, up_ref, gain_ref, rms_ref, out_ref, low_ref,
+    inbox, stats, send, recv, stat_send, stat_recv, own_sem,
+):
+    d, sec, t = lax.axis_index("dp"), lax.axis_index("section"), lax.axis_index("tensor")
+    many, wide = x_ref.shape
+    tile = 16
+    for k in range(1, n):
+        greet(at(d, sec, lax.rem(t + k, n)))
+    pl.semaphore_wait(pltpu.get_barrier_semaphore(), n - 1)
+
+    def block(j):
+        return part_ref.at[:, pl.ds(pl.multiple_of(j * wide, wide), wide)]
+
+    @pl.when(sec == active)
+    def _():
+        own = pltpu.make_async_copy(block(t), inbox.at[t], own_sem)
+        own.start()
+
+        def push(k):
+            peer = lax.rem(t + k, n)
+            return remote(
+                block(peer), inbox.at[t], send.at[k], recv.at[t], at(d, sec, peer)
+            )
+
+        for k in range(1, n):
+            push(k).start()
+        own.wait()
+        for k in range(1, n):
+            peer = lax.rem(t + k, n)
+            remote(
+                block(peer), inbox.at[peer], send.at[k], recv.at[peer], at(d, sec, peer)
+            ).wait_recv()
+
+        def gather_sum(index, carry):
+            rows = pl.ds(pl.multiple_of(index * tile, tile), tile)
+            total = inbox[0, rows, :].astype(F32)
+            for j in range(1, n):
+                total = total + inbox[j, rows, :].astype(F32)
+            scaled = total * gain_ref[...]
+            out_ref[rows, :] = scaled
+            dots = jnp.sum(x_ref[rows, :].astype(F32) * scaled, -1, keepdims=True)
+            stats[t, rows, :] = jnp.broadcast_to(dots, (tile, HD))
+            return carry
+
+        lax.fori_loop(0, many // tile, gather_sum, 0)
+
+        for k in range(1, n):
+            peer = lax.rem(t + k, n)
+            remote(
+                stats.at[t], stats.at[t], stat_send.at[k], stat_recv.at[t], at(d, sec, peer)
+            ).start()
+        for k in range(1, n):
+            peer = lax.rem(t + k, n)
+            remote(
+                stats.at[peer], stats.at[peer], stat_send.at[k], stat_recv.at[peer],
+                at(d, sec, peer),
+            ).wait_recv()
+
+        def settle(index, carry):
+            rows = pl.ds(pl.multiple_of(index * tile, tile), tile)
+            stat = stats[0, rows, :]
+            for j in range(1, n):
+                stat = stat + stats[j, rows, :]
+            rms = rms_ref[rows, :]
+            factor = (rms * rms * rms * stat / width)[:, :1]
+            value = (
+                up_ref[rows, :].astype(F32)
+                + rms[:, :1] * out_ref[rows, :]
+                - x_ref[rows, :].astype(F32) * factor
+            )
+            out_ref[rows, :] = value
+            low_ref[rows, :] = value.astype(BF16)
+            return carry
+
+        lax.fori_loop(0, many // tile, settle, 0)
+        for k in range(1, n):
+            push(k).wait_send()
+            peer = lax.rem(t + k, n)
+            remote(
+                stats.at[t], stats.at[t], stat_send.at[k], stat_recv.at[t], at(d, sec, peer)
+            ).wait_send()
+
+
+def finish(n, active, part, x, up, gain, rms):
+    many, wide = x.shape
+    dma = pltpu.SemaphoreType.DMA
+    vmem = pl.BlockSpec(memory_space=pltpu.VMEM)
+    return pl.pallas_call(
+        functools.partial(finish_body, n, active, part.shape[1]),
+        in_specs=[pl.BlockSpec(memory_space=pl.ANY)] + [vmem] * 4,
+        out_specs=[vmem, vmem],
+        out_shape=[
+            jax.ShapeDtypeStruct((many, wide), F32),
+            jax.ShapeDtypeStruct((many, wide), BF16),
+        ],
+        scratch_shapes=[
+            pltpu.VMEM((n, many, wide), BF16),
+            pltpu.VMEM((n, many, HD), F32),
+            dma((n,)),
+            dma((n,)),
+            dma((n,)),
+            dma((n,)),
+            dma,
+        ],
+        compiler_params=pltpu.CompilerParams(
+            collective_id=1 + active, has_side_effects=True, vmem_limit_bytes=BIG
+        ),
+    )(part, x, up, gain, rms)
+
+
+def descend_body(
+    n, g_ref, w_ref, up_out, go_out, mid, spread, w_in, outbox, inbox,
+    g_send, g_recv, s_send, s_recv, p_send, p_recv, w_sem, up_sem,
+):
+    d, sec, t = lax.axis_index("dp"), lax.axis_index("section"), lax.axis_index("tensor")
+    for k in range(n):
+        greet(at(d, 1 - sec, lax.rem(t + k, n)))
+
+    @pl.when(sec == 0)
+    def _():
+        for k in range(1, n):
+            greet(at(lax.rem(d + k, n), sec, t))
+
+    pl.semaphore_wait(pltpu.get_barrier_semaphore(), n + (1 - sec) * (n - 1))
+
+    def hand(k):
+        return remote(
+            g_ref, mid.at[t], g_send.at[k], g_recv.at[t], at(d, 0, lax.rem(t + k, n))
+        )
+
+    @pl.when(sec == 1)
+    def _():
+        for k in range(n):
+            hand(k).start()
+        for k in range(n):
+            hand(k).wait_send()
+
+    @pl.when(sec == 0)
+    def _():
+        load = pltpu.make_async_copy(w_ref, w_in, w_sem)
+        load.start()
+
+        def arrived(slot):
+            remote(
+                mid.at[slot], mid.at[slot], g_send.at[0], g_recv.at[slot], at(d, 1, slot)
+            ).wait_recv()
+
+        def move(k):
+            peer = lax.rem(d + k, n)
+            return remote(
+                mid.at[peer], spread.at[d], s_send.at[k], s_recv.at[d], at(peer, 0, t)
+            )
+
+        for k in range(1, n):
+            arrived(lax.rem(d + k, n))
+            move(k).start()
+        arrived(d)
+        keep = pltpu.make_async_copy(mid.at[t], up_out, up_sem)
+        keep.start()
+        load.wait()
+
+        def give(k):
+            peer = lax.rem(d + k, n)
+            return remote(
+                outbox.at[peer], inbox.at[d], p_send.at[k], p_recv.at[d], at(peer, 0, t)
+            )
+
+        for k in range(1, n):
+            peer = lax.rem(d + k, n)
+            remote(
+                spread.at[peer], spread.at[peer], s_send.at[k], s_recv.at[peer],
+                at(peer, 0, t),
+            ).wait_recv()
+
+            def store(start, size, value):
+                outbox[peer, :, pl.ds(start, size)] = value
+
+            tiled_dot_t(spread.at[peer], w_in, store)
+            give(k).start()
+
+        def store_own(start, size, value):
+            outbox[d, :, pl.ds(start, size)] = value
+
+        tiled_dot_t(mid.at[d], w_in, store_own)
+        for k in range(1, n):
+            peer = lax.rem(d + k, n)
+            remote(
+                inbox.at[peer], inbox.at[peer], p_send.at[k], p_recv.at[peer],
+                at(peer, 0, t),
+            ).wait_recv()
+        tile = 16
+
+        def add(index, carry):
+            rows = pl.ds(pl.multiple_of(index * tile, tile), tile)
+            total = outbox[d, rows, :].astype(F32)
+            for k in range(1, n):
+                total = total + inbox[lax.rem(d + k, n), rows, :].astype(F32)
+            go_out[rows, :] = total.astype(BF16)
+            return carry
+
+        lax.fori_loop(0, go_out.shape[0] // tile, add, 0)
+        keep.wait()
+        for k in range(1, n):
+            move(k).wait_send()
+            give(k).wait_send()
+
+
+def descend(n, g, w):
+    many, wide = g.shape
+    cols = w.shape[0]
+    dma = pltpu.SemaphoreType.DMA
+    vmem = pl.BlockSpec(memory_space=pltpu.VMEM)
+    return pl.pallas_call(
+        functools.partial(descend_body, n),
+        in_specs=[vmem, pl.BlockSpec(memory_space=pl.ANY)],
+        out_specs=[vmem, vmem],
+        out_shape=[
+            jax.ShapeDtypeStruct((many, wide), BF16),
+            jax.ShapeDtypeStruct((many, cols), BF16),
+        ],
+        scratch_shapes=[
+            pltpu.VMEM((n, many, wide), BF16),
+            pltpu.VMEM((n, many, wide), BF16),
+            pltpu.VMEM(w.shape, BF16),
+            pltpu.VMEM((n, many, cols), BF16),
+            pltpu.VMEM((n, many, cols), BF16),
+            dma((n,)),
+            dma((n,)),
+            dma((n,)),
+            dma((n,)),
+            dma((n,)),
+            dma((n,)),
+            dma,
+            dma,
+        ],
+        compiler_params=pltpu.CompilerParams(
+            collective_id=3, has_side_effects=True, vmem_limit_bytes=BIG
+        ),
+    )(g, w)
+
+
 def on_device(
-    n_dp, n_tensor, stored, cotangent, positions, lengths, norm_gain, w_query, w_key, w_value, w_out
+    n_tensor, stored, cotangent, positions, lengths, norm_gain, w_query, w_key, w_value, w_out
 ):
     x_own = stored[0]
     gain = norm_gain[0]
@@ -122,27 +556,38 @@
     dp_id = lax.axis_index("dp")
     tensor_id = lax.axis_index("tensor")
     section_id = lax.axis_index("section")
-    swap = [(d * n_tensor + t, t * n_tensor + d) for d in range(n_dp) for t in range(n_tensor)]
-
     row_ids = dp_id * rows + jnp.arange(rows, dtype=jnp.int32)
     cosine, sine = angle_tables(row_ids.astype(F32))
     lens = jnp.stack(
         [lengths, jnp.full_like(lengths, dp_id * rows)], 0
     )
 
-    cot_slice = lax.ppermute(cotangent, ("dp", "tensor"), swap)
     resp = cotangent.shape[1]
-    resp_part = dot_t(cot_slice.reshape(seqs * resp, width_dev), w_o)
-    resp_grad = lax.psum(resp_part.astype(BF16), "dp").reshape(seqs, resp, -1)
+    x_parts, resp_grad = opening(
+        n_tensor,
+        x_own.reshape(many, width_dev),
+        cotangent.reshape(seqs * resp, width_dev),
+        w_o,
+    )
+    resp_grad = resp_grad.reshape(seqs, resp, -1)
     placed = (positions[:, None, :] == row_ids[None, :, None]).astype(BF16)
 
     def place(small):
         return jnp.einsum("spr,srd->spd", placed, small, preferred_element_type=F32).astype(BF16)
 
-    x_whole = lax.all_gather(x_own, "tensor", axis=2, tiled=True)
-    x_full = x_whole.astype(F32)
-    inv_rms = lax.rsqrt(jnp.mean(x_full * x_full, -1, keepdims=True) + EPS)
-    normed = (x_full * inv_rms * gain).astype(BF16).reshape(many, width)
+    squares = jnp.sum(jnp.square(x_parts.astype(F32)), (0, 2))[:, None]
+    inv_rms = lax.rsqrt(squares / width + EPS)
+    normed = jnp.concatenate(
+        [
+            (
+                x_parts[part].astype(F32)
+                * inv_rms
+                * gain[part * width_dev : (part + 1) * width_dev]
+            ).astype(BF16)
+            for part in range(n_tensor)
+        ],
+        1,
+    )
     queries, keys, values = lax.optimization_barrier(
         (dot_n(normed, w_q), dot_n(normed, w_k), dot_n(normed, w_v))
     )
@@ -155,9 +600,10 @@
     k_all, v_all = kv_all[..., :kv_cols], kv_all[..., kv_cols:]
     queries = queries.reshape(seqs, rows, -1)
     gain_own = lax.dynamic_slice_in_dim(gain, tensor_id * width_dev, width_dev, 0)
-    x_mine = x_own.astype(F32)
-
-    def backward(upstream_own, grad_out):
+    x_mine = x_own.reshape(many, width_dev)
+    rms_wide = jnp.broadcast_to(inv_rms, (many, HD))
+
+    def backward(active, upstream_own, grad_out):
         grad_q, key_terms, value_terms = attention_grad(
             lens, queries, grad_out, k_all, v_all, cosine, sine
         )
@@ -169,38 +615,27 @@
         grad_k = grad_k.astype(BF16).reshape(many, kv_cols)
         grad_v = kv_sum[..., kv_cols:].astype(BF16).reshape(many, kv_cols)
         partial = dot_t(grad_q.reshape(many, -1), w_q) + dot_t(grad_k, w_k) + dot_t(grad_v, w_v)
-        summed = lax.psum_scatter(
-            partial.astype(BF16), "tensor", scatter_dimension=1, tiled=True
-        ).astype(F32)
-        summed = summed.reshape(seqs, rows, width_dev)
-        stat = lax.psum(jnp.sum(x_mine * gain_own * summed, -1, keepdims=True), "tensor")
-        return (
-            upstream_own.astype(F32)
-            + inv_rms * gain_own * summed
-            - x_mine * inv_rms**3 * stat / width
+        return finish(
+            n_tensor,
+            active,
+            partial.astype(BF16),
+            x_mine,
+            upstream_own.reshape(many, width_dev),
+            gain_own[None],
+            rms_wide,
         )
 
-    first = backward(place(cotangent), place(resp_grad))
-
-    first_b = first.astype(BF16)
-    down = [(1, 0)]
-    handed = lax.ppermute(first_b, "section", down)
-    across = [
-        ((d * 2 + 1) * n_tensor + t, (t * 2) * n_tensor + d)
-        for d in range(n_dp)
-        for t in range(n_tensor)
-    ]
-    crossed = lax.ppermute(first_b, ("dp", "section", "tensor"), across)
-    up_rows = lax.all_gather(crossed, "tensor", axis=0, tiled=False)
-    up_part = dot_t(up_rows.reshape(n_dp * many, width_dev), w_o).astype(BF16)
-    grad_out = lax.psum_scatter(up_part, "dp", scatter_dimension=0, tiled=True)
-    second = backward(handed, grad_out.reshape(seqs, rows, -1))
-    return jnp.where(section_id == 0, second, first)[None]
+    first, first_low = backward(1, place(cotangent), place(resp_grad))
+
+    handed, grad_out = descend(n_tensor, first_low, w_o)
+    second, _ = backward(0, handed, grad_out.reshape(seqs, rows, -1))
+    result = jnp.where(section_id == 0, second, first)
+    return result.reshape(1, seqs, rows, width_dev)
 
 
 def solution(mesh):
     return jax.shard_map(
-        functools.partial(on_device, mesh.shape["dp"], mesh.shape["tensor"]),
+        functools.partial(on_device, mesh.shape["tensor"]),
         mesh=mesh,
         in_specs=(
             P("section", None, "dp", "tensor"),

time: 432 us -> 341 us (0.79)
  waiting for transfers between devices: 264 us -> 19.7 us
  Pallas kernels: 9.74 us -> 207 us
  matrix products: 86 us -> 66.9 us
  blocking collectives: 30.2 us -> 13.9 us
  starting transfers between devices: 4.87 us -> 0.22 us
    pallas_call x0 -> x4, Pallas kernels: none -> 198 us  [the longest x1 83.6 us: descend(): pl.pallas_call(functools.partial(descend_body, n), in_specs=[vmem, pl.Blo...]
    reduce_scatter x3 -> x0, waiting for transfers between devices: 120 us -> none  [the longest x2 85.8 us: backward(): lax.psum_scatter(partial.astype(BF16), 'tensor', scatter_dimension=1, til...]
    all_gather x2 -> x0, waiting for transfers between devices: 64.7 us -> none  [the longest x1 61.5 us: on_device(): up_rows = lax.all_gather(crossed, 'tensor', axis=0, tiled=False)]
    psum x1 -> x0, waiting for transfers between devices: 64.5 us -> none  [on_device(): resp_grad = lax.psum(resp_part.astype(BF16), 'dp').reshape(seqs, resp, -1)]
    psum x2 -> x0, blocking collectives: 20.2 us -> none  [backward(): lax.psum(jnp.sum(x_mine * gain_own * summed, -1, keepdims=True), 'tensor')]
    dot_general x8 -> x6, matrix products: 67.6 us -> 50.8 us  [dot_t(): lax.dot_general(left, right, (((1,), (1,)), ((), ())), preferred_element_...]
    reduce_scatter x2, waiting for transfers between devices: 12.2 us -> 19.7 us  [backward(): lax.psum_scatter(jnp.concatenate([key_terms, value_terms], -1), 'dp', sca...]
  transfers between devices with their start and end apart: 11 -> 2, of which waited for: 9 -> 2; matrix products, arithmetic and copies ran while one was open for 9% -> 11% of each run, Pallas kernels for 0% -> 0%
where the time goes in v2:
time: 341 us; the launch traced here: 340 us
  Pallas kernels  207 us (61%)
  matrix products  66.9 us (20%)
  waiting for transfers between devices  19.7 us (6%)
  blocking collectives  13.9 us (4%)
  between operations  13.8 us (4%)
  other arithmetic  13 us (4%)
  local copies, waits for them, and re-layouts  5.04 us (1%)
    pallas_call x1, Pallas kernels, descend(): pl.pallas_call(functools.partial(descend_body, n), in_specs=[vmem, pl.Blo...  83.6 us
    pallas_call x1, Pallas kernels, opening(): pl.pallas_call(functools.partial(opening_body, n), in_specs=[pl.BlockSpec...  69.7 us
    dot_general x6, matrix products, dot_t(): lax.dot_general(left, right, (((1,), (1,)), ((), ())), preferred_element_...  50.8 us
    pallas_call x2, Pallas kernels, finish(): pl.pallas_call(functools.partial(finish_body, n, active, part.shape[1]),...  44.4 us
    reduce_scatter x2, waiting for transfers between devices, backward(): lax.psum_scatter(jnp.concatenate([key_terms, value_terms], -1), 'dp', sca...  19.7 us
    dot_general x3, matrix products, dot_n(): lax.dot_general(left, right, (((1,), (0,)), ((), ())), preferred_element_...  14.5 us
    all_gather x1, blocking collectives, on_device(): kv_all = lax.all_gather(kv_own, 'dp', axis=1, tiled=True)  13.9 us
    pallas_call x2, Pallas kernels, attention_grad(): pl.pallas_call(attention_body, grid=(batch, kv_dev), in_specs=[pl.BlockSp...  9.74 us
  transfers between devices with their start and end apart: 2, of which 2 were waited for; matrix products, arithmetic and copies ran while one was open for 11% of the time, Pallas kernels for 0%

profile of v2, /device:TPU:0, one launch (start us, length us, event | category | flops | bytes accessed | tf_op | source)
XLA Modules:
  0.0 340.0 jit_solution(13904100570764341940)
XLA Ops:
  6.5 0.0 reduce-scatter.3.cloned.1.call-start
  6.6 0.0 copy-start.8
  6.6 69.7 %shard_map.91 = (bf16[4,128,2048]{2,1,0:T(8,128)(2,1)}, bf16[64,2048]{1,0:T(8,128)(2,1)}) custom-call(bf16[128,2048]{1,0:T(8,128)(2,1)} %bitcast.77, bf16[64,2048]{1,0:T(8,128)(2,1)} %bitcast.81, bf16[2048,2048]{1,0:T(8,128)(2,1)} %bitcast.75), custom_call_target="tpu_custom_call" | custom-call | tf_op jit(solution)/shard_map/pallas_call | solution.py:273
  76.3 2.1 multiply_reduce_fusion
  78.4 0.0 copy-done.8
  78.4 0.0 copy-start.2
  78.4 0.6 constant_dynamic-slice_fusion
  79.0 2.4 fusion.23
  81.5 0.0 copy-done.2
  81.5 0.0 copy-start.1
  81.5 0.8 fusion.10
  82.3 1.4 copy-done.1
  83.7 0.8 fusion.14
  84.4 13.0 %fusion.4 = f32[128,2048]{1,0:T(8,128)S(1)} fusion(bf16[1,8192,2048]{2,1,0:T(8,128)(2,1)} %param.14, bf16[128,2048]{1,0:T(8,128)(2,1)S(1)} %get-tuple-element.40, bf16[128,2048]{1,0:T(8,128)(2,1)S(1)} %get-tuple-element.39, bf16[128,2048]{1,0:T(8,128)(2,1)S(1)} %get-tuple-element.38, bf16[128,2048]{1,0:T(8,128)(2,1)S(1)} %get-tuple-element.37), kind=kOutput, calls=%fused_computation.4 | convolution fusion | flops 4303355904 | bytes 36700160 | tf_op jit(solution)/shard_map/dot_general | solution.py:23
  97.5 0.0 copy-start.10
  97.5 0.0 copy-start.7
  97.5 0.0 copy-start.9
  97.5 0.1 reshape.121
  97.6 0.2 fusion.37
  97.8 0.0 copy-start.5
  97.8 0.2 pad_maximum_fusion.3
  98.0 0.1 concatenate.37
  98.1 0.2 multiply_cosine_fusion
  98.3 0.1 pad_maximum_fusion.7
  98.5 13.9 %all_gather.3 = bf16[2,256,512]{2,1,0:T(8,128)(2,1)S(1)} all-gather(bf16[2,64,512]{2,1,0:T(8,128)(2,1)S(1)} %pad_maximum_fusion.4), channel_id=1, replica_groups=mesh['dp'=4,'section'=2,'tensor'=4] {'dp'}, dimensions={1}, use_global_device_ids=true | all-gather | bytes 655360 | tf_op jit(solution)/shard_map/all_gather | solution.py:599
  112.5 0.0 copy-done.10
  112.5 0.0 copy-done.7
  112.6 0.4 convolution_convert_fusion.1.o_ref
  113.0 4.9 %shard_map.92 = (bf16[2,64,2048]{2,1,0:T(8,128)(2,1)S(1)}, bf16[2,256,256]{2,1,0:T(8,128)(2,1)S(1)}, bf16[2,256,256]{2,1,0:T(8,128)(2,1)S(1)}) custom-call(s32[2,2]{1,0:T(2,128)S(1)} %stack.7.lens_ref, f32[2,64,2048]{2,1,0:T(8,128)S(1)} %bitcast.70, bf16[2,64,2048]{2,1,0:T(8,128)(2,1)S(1)} %convolution_convert_fusion.1.o_ref, ...), custom_call_target="tpu_custom_call" | custom-call | tf_op jit(solution)/shard_map/pallas_call | solution.py:90
  117.9 0.8 pad_maximum_fusion.1
  118.7 0.0 reduce-scatter.3.cloned.1.call-update
  118.7 0.2 reduce-scatter.5.cloned.1.call-start
  119.0 1.2 convolution_convert_fusion
  120.2 17.4 %fusion.2 = f32[128,8192]{1,0:T(8,128)} fusion(bf16[128,2048]{1,0:T(8,128)(2,1)S(1)} %bitcast.72, bf16[1,8192,2048]{2,1,0:T(8,128)(2,1)} %param.14), kind=kOutput, calls=%fused_computation.2 | convolution fusion | flops 4294967296 | bytes 38273024 | tf_op jit(solution)/shard_map/dot_general | solution.py:19
  137.6 5.0 %reduce-scatter.3.cloned.1.call-done = bf16[2,64,512]{2,1,0:T(8,128)(2,1)} async-done(((bf16[2,256,512]{2,1,0:T(8,128)(2,1)}), bf16[2,64,512]{2,1,0:T(8,128)(2,1)}) %reduce-scatter.3.cloned.1.call-update) | async-done | bytes 131088 | tf_op jit(solution)/shard_map/reduce_scatter | solution.py:610
  142.6 0.9 fusion.35
  143.5 0.1 reshape.124
  143.6 0.2 fusion.36
  143.8 0.2 pad_maximum_fusion.5
  144.0 0.1 concatenate.42
  144.1 0.9 subtract_convert_fusion.1
  145.0 0.0 copy-start.3
  145.0 5.1 %convolution_add_fusion.3 = f32[128,8192]{1,0:T(8,128)S(1)} fusion(f32[128,8192]{1,0:T(8,128)} %fusion.2, bf16[128,256]{1,0:T(8,128)(2,1)S(1)} %bitcast.92, bf16[1,8192,256]{2,1,0:T(8,128)(2,1)} %param.15), kind=kOutput, calls=%fused_computation.9 | convolution fusion | flops 537919488 | bytes 12648448 | tf_op jit(solution)/shard_map/dot_general | solution.py:19
  150.2 2.9 fusion.6.part_ref
  153.0 0.7 broadcast_in_dim.2.rms_ref
  153.7 5.8 %shard_map.93 = (f32[128,2048]{1,0:T(8,128)}, bf16[128,2048]{1,0:T(8,128)(2,1)}) custom-call(bf16[128,8192]{1,0:T(8,128)(2,1)} %fusion.6.part_ref, bf16[128,2048]{1,0:T(8,128)(2,1)} %bitcast.78, bf16[128,2048]{1,0:T(8,128)(2,1)} %bitcast.80, f32[1,2048]{1,0:T(1,128)} %get-tuple-element.53.gain_ref, f32[128,128]{1,0:T(8,128)} %broadcast_in_dim.2.rms_ref), custom_call_target="tpu_custom_call" | custom-call | tf_op jit(solution)/shard_map/pallas_call | solution.py:392
  159.6 83.6 %shard_map.94 = (bf16[128,2048]{1,0:T(8,128)(2,1)}, bf16[128,2048]{1,0:T(8,128)(2,1)}) custom-call(bf16[128,2048]{1,0:T(8,128)(2,1)} %get-tuple-element.29.g_ref, bf16[2048,2048]{1,0:T(8,128)(2,1)} %bitcast.76), custom_call_target="tpu_custom_call" | custom-call | tf_op jit(solution)/shard_map/pallas_call | solution.py:517
  243.1 1.0 copy-done
  244.2 4.9 %shard_map.95 = (bf16[2,64,2048]{2,1,0:T(8,128)(2,1)S(1)}, bf16[2,256,256]{2,1,0:T(8,128)(2,1)S(1)}, bf16[2,256,256]{2,1,0:T(8,128)(2,1)S(1)}) custom-call(s32[2,2]{1,0:T(2,128)S(1)} %stack.7.lens_ref, f32[2,64,2048]{2,1,0:T(8,128)S(1)} %bitcast.71, bf16[2,64,2048]{2,1,0:T(8,128)(2,1)S(1)} %bitcast.74, bf16[2,256,256]{2,1,0:T(8,128)(2,1)S(1)} %get-tuple-element.42.k_ref, ...), custom_call_target="tpu_custom_call" | custom-call | tf_op jit(solution)/shard_map/pallas_call | solution.py:90
  249.0 0.8 pad_maximum_fusion.2
  249.9 0.0 reduce-scatter.5.cloned.1.call-update
  249.9 17.4 %fusion = f32[128,8192]{1,0:T(8,128)} fusion(bf16[128,2048]{1,0:T(8,128)(2,1)S(1)} %bitcast.73, bf16[1,8192,2048]{2,1,0:T(8,128)(2,1)} %param.14), kind=kOutput, calls=%fused_computation | convolution fusion | flops 4294967296 | bytes 38273024 | tf_op jit(solution)/shard_map/dot_general | solution.py:19
  267.3 14.7 %reduce-scatter.5.cloned.1.call-done = bf16[2,64,512]{2,1,0:T(8,128)(2,1)} async-done(((bf16[2,256,512]{2,1,0:T(8,128)(2,1)}), bf16[2,64,512]{2,1,0:T(8,128)(2,1)}) %reduce-scatter.5.cloned.1.call-update) | async-done | bytes 131088 | tf_op jit(solution)/shard_map/reduce_scatter | solution.py:610
  281.9 0.9 fusion.33
  282.8 0.1 reshape.129
  282.9 0.2 fusion.34
  283.1 0.2 pad_maximum_fusion.6
  283.3 0.1 concatenate.45
  283.4 0.9 subtract_convert_fusion
  284.3 0.0 copy-start.4
  284.3 5.1 %convolution_add_fusion.1 = f32[128,8192]{1,0:T(8,128)S(1)} fusion(f32[128,8192]{1,0:T(8,128)} %fusion, bf16[128,256]{1,0:T(8,128)(2,1)S(1)} %bitcast.91, bf16[1,8192,256]{2,1,0:T(8,128)(2,1)} %param.15), kind=kOutput, calls=%fused_computation.7 | convolution fusion | flops 537919488 | bytes 12648448 | tf_op jit(solution)/shard_map/dot_general | solution.py:19
  289.4 2.9 fusion.7.part_ref
  292.3 38.5 %shard_map.96 = (f32[128,2048]{1,0:T(8,128)}, bf16[128,2048]{1,0:T(8,128)(2,1)}) custom-call(bf16[128,8192]{1,0:T(8,128)(2,1)} %fusion.7.part_ref, bf16[128,2048]{1,0:T(8,128)(2,1)} %bitcast.79, bf16[128,2048]{1,0:T(8,128)(2,1)} %get-tuple-element.34.up_ref, f32[1,2048]{1,0:T(1,128)} %get-tuple-element.53.gain_ref, f32[128,128]{1,0:T(8,128)} %broadcast_in_dim.2.rms_ref), custom_call_target="tpu_custom_call" | custom-call | tf_op jit(solution)/shard_map/pallas_call | solution.py:392
  330.9 2.3 broadcast_select_fusion
  (19 shorter events, 0.2 us)
Async XLA Ops:
  6.5 136.1 %reduce-scatter.3.cloned.1.call-start = ((), (), s32[]{:S(2)}) async-start(), calls=%async_computation.2 | async-start | bytes 655360 | tf_op jit(solution)/shard_map/reduce_scatter | solution.py:610
  6.6 71.8 %copy-start.8 = (f32[1,8192]{1,0:T(1,128)S(1)}, f32[1,8192]{1,0:T(1,128)}, u32[]{:S(2)}) copy-start(f32[1,8192]{1,0:T(1,128)} %param.13) | copy-start | bytes 98308
  78.4 3.1 copy-start.2
  81.5 2.2 copy-start.1
  97.5 15.1 %copy-start.10 = (s32[2]{0:T(128)S(1)}, s32[2]{0:T(128)}, u32[]{:S(2)}) copy-start(s32[2]{0:T(128)} %param.12) | copy-start | bytes 28
  97.5 15.1 %copy-start.7 = (bf16[64,2048]{1,0:T(8,128)(2,1)S(1)}, bf16[64,2048]{1,0:T(8,128)(2,1)}, u32[]{:S(2)}) copy-start(bf16[64,2048]{1,0:T(8,128)(2,1)} %get-tuple-element.23) | copy-start | bytes 786436
  97.5 15.1 %copy-start.9 = (s32[2,32]{1,0:T(2,128)S(1)}, s32[2,32]{1,0:T(2,128)}, u32[]{:S(2)}) copy-start(s32[2,32]{1,0:T(2,128)} %param.11) | copy-start | bytes 772
  97.8 21.2 %copy-start.5 = (bf16[2,32,2048]{2,1,0:T(8,128)(2,1)S(1)}, bf16[2,32,2048]{2,1,0:T(8,128)(2,1)}, u32[]{:S(2)}) copy-start(bf16[2,32,2048]{2,1,0:T(8,128)(2,1)} %param.10) | copy-start | bytes 786436
  118.7 163.2 %reduce-scatter.5.cloned.1.call-start = ((), (), s32[]{:S(2)}) async-start(), calls=%async_computation.3 | async-start | bytes 655360 | tf_op jit(solution)/shard_map/reduce_scatter | solution.py:610
  145.0 5.1 %copy-start.3 = (bf16[1,8192,256]{2,1,0:T(8,128)(2,1)S(1)}, bf16[1,8192,256]{2,1,0:T(8,128)(2,1)}, u32[]{:S(2)}) copy-start(bf16[1,8192,256]{2,1,0:T(8,128)(2,1)} %param.16) | copy-start | bytes 12582916
  243.1 1.0 copy-start
  284.3 5.1 %copy-start.4 = (bf16[1,8192,256]{2,1,0:T(8,128)(2,1)S(1)}, bf16[1,8192,256]{2,1,0:T(8,128)(2,1)}, u32[]{:S(2)}) copy-start(bf16[1,8192,256]{2,1,0:T(8,128)(2,1)} %param.16) | copy-start | bytes 12582916
  289.4 41.4 %copy-start.6 = (f32[128,2048]{1,0:T(8,128)S(1)}, f32[128,2048]{1,0:T(8,128)}, u32[]{:S(2)}) copy-start(f32[128,2048]{1,0:T(8,128)} %get-tuple-element.36) | copy-start | bytes 3145732
Sparse Core Ops, SparseCore 0:
  118.9 23.7 reduce-scatter.2
  250.0 31.8 reduce-scatter.4

commit v3 on v2

--- a/solution.py
+++ b/solution.py
@@ -39,74 +39,6 @@
 def turn_plain(values):
     half_dim = HD // 2
     return jnp.concatenate([values[..., half_dim:], values[..., :half_dim]], -1)
-
-
-def attention_body(lens_ref, q_ref, o_ref, k_ref, v_ref, cos_ref, sin_ref, gq_ref, gk_ref, gv_ref):
-    seq = pl.program_id(0)
-    rows = q_ref.shape[1]
-    length = k_ref.shape[1]
-    group = q_ref.shape[2] // HD
-    scale = 1.0 / math.sqrt(HD)
-    cosine, sine = cos_ref[...], sin_ref[...]
-    q_parts, o_parts = [], []
-    for head in range(group):
-        lanes = slice(head * HD, (head + 1) * HD)
-        raw = q_ref[0, :, lanes]
-        q_parts.append((raw * cosine + pltpu.roll(raw, HD // 2, 1) * sine).astype(BF16))
-        o_parts.append(o_ref[0, :, lanes])
-    q_all = jnp.concatenate(q_parts, 0)
-    o_all = jnp.concatenate(o_parts, 0)
-    keys, values = k_ref[0], v_ref[0]
-    many = rows * group
-    row_at = lax.broadcasted_iota(jnp.int32, (many, length), 0) & (rows - 1)
-    query_at = lens_ref[1, 0] + row_at
-    key_at = lax.broadcasted_iota(jnp.int32, (many, length), 1)
-    start = length - lens_ref[0, seq]
-    allowed = (key_at == query_at) | ((key_at < query_at) & (key_at >= start))
-    scores = jnp.where(allowed, dot_t(q_all, keys) * scale, -1e30)
-    highest = jnp.max(scores, -1, keepdims=True)
-    terms = jnp.where(allowed, jnp.exp(scores - highest), 0.0)
-    probs = terms / jnp.sum(terms, -1, keepdims=True)
-    grad_probs = dot_t(o_all, values)
-    row_dot = jnp.sum(probs * grad_probs, -1, keepdims=True)
-    grad_scores = (probs * (grad_probs - row_dot) * scale).astype(BF16)
-    grad_qr = dot_n(grad_scores, keys)
-    gk_ref[0] = dot_c(grad_scores, q_all).astype(BF16)
-    gv_ref[0] = dot_c(probs.astype(BF16), o_all).astype(BF16)
-    for head in range(group):
-        part = grad_qr[head * rows : (head + 1) * rows]
-        turned = part * cosine - pltpu.roll(part, HD // 2, 1) * sine
-        gq_ref[0, :, head * HD : (head + 1) * HD] = turned.astype(BF16)
-
-
-def attention_grad(lens, queries, grad_out, keys, values, cosine, sine):
-    batch, rows, cols = queries.shape
-    length = keys.shape[1]
-    kv_dev = keys.shape[2] // HD
-    group_cols = cols // kv_dev
-    q_spec = pl.BlockSpec((1, rows, group_cols), lambda b, h: (b, 0, h))
-    k_spec = pl.BlockSpec((1, length, HD), lambda b, h: (b, 0, h))
-    t_spec = pl.BlockSpec((rows, HD), lambda b, h: (0, 0))
-    return pl.pallas_call(
-        attention_body,
-        grid=(batch, kv_dev),
-        in_specs=[
-            pl.BlockSpec(memory_space=pltpu.SMEM),
-            q_spec,
-            q_spec,
-            k_spec,
-            k_spec,
-            t_spec,
-            t_spec,
-        ],
-        out_specs=[q_spec, k_spec, k_spec],
-        out_shape=[
-            jax.ShapeDtypeStruct((batch, rows, cols), BF16),
-            jax.ShapeDtypeStruct((batch, length, kv_dev * HD), BF16),
-            jax.ShapeDtypeStruct((batch, length, kv_dev * HD), BF16),
-        ],
-        compiler_params=pltpu.CompilerParams(vmem_limit_bytes=32 * 1024 * 1024),
-    )(lens, queries, grad_out, keys, values, cosine, sine)
 
 
 MESH = pl.DeviceIdType.MESH
@@ -185,21 +117,29 @@
     def _():
         pass_on(x_ref, t, False).start()
 
+    load = pltpu.make_async_copy(w_ref, w_in, w_sem)
+    swap = remote(cot_ref, cot_in, cot_sems.at[0], cot_sems.at[1], at(t, sec, d))
+    keep = pltpu.make_async_copy(cot_ref, cot_in, cot_sems.at[2])
+
     @pl.when(sec == 1)
     def _():
-        load = pltpu.make_async_copy(w_ref, w_in, w_sem)
         load.start()
-        swap = remote(cot_ref, cot_in, cot_sems.at[0], cot_sems.at[1], at(t, sec, d))
-        keep = pltpu.make_async_copy(cot_ref, cot_in, cot_sems.at[2])
 
         @pl.when(d != t)
         def _():
             swap.start()
-            swap.wait()
 
         @pl.when(d == t)
         def _():
             keep.start()
+
+    def respond():
+        @pl.when(d != t)
+        def _():
+            swap.wait()
+
+        @pl.when(d == t)
+        def _():
             keep.wait()
 
         load.wait()
@@ -232,6 +172,9 @@
             @pl.when(t > 0)
             def _():
                 pass_on(x_out.at[right], right, False).start()
+
+        if k == 1:
+            pl.when(sec == 1)(respond)
 
     own.wait()
 
@@ -302,37 +245,76 @@
 
 
 def finish_body(
-    n, active, width, part_ref, x_ref, up_ref, gain_ref, rms_ref, out_ref, low_ref,
-    inbox, stats, send, recv, stat_send, stat_recv, own_sem,
+    n, active, width, gq_ref, gkv_ref, x_ref, up_ref, gain_ref, rms_ref, wq_ref, wk_ref, wv_ref,
+    out_ref, low_ref, inbox, outbox, stats, wq_in, wk_in, wv_in, w_sems,
+    send, recv, stat_send, stat_recv,
 ):
     d, sec, t = lax.axis_index("dp"), lax.axis_index("section"), lax.axis_index("tensor")
     many, wide = x_ref.shape
+    kv_cols = wk_in.shape[2]
     tile = 16
+    deep = wq_in.shape[1]
+    per = wide // deep
+
     for k in range(1, n):
         greet(at(d, sec, lax.rem(t + k, n)))
     pl.semaphore_wait(pltpu.get_barrier_semaphore(), n - 1)
 
-    def block(j):
-        return part_ref.at[:, pl.ds(pl.multiple_of(j * wide, wide), wide)]
-
     @pl.when(sec == active)
     def _():
-        own = pltpu.make_async_copy(block(t), inbox.at[t], own_sem)
-        own.start()
+        def loads(count):
+            owner = lax.rem(t + 1 + count // per, n)
+            rows = pl.ds(pl.multiple_of(owner * wide + lax.rem(count, per) * deep, deep), deep)
+            slot = lax.rem(count, 2)
+            return [
+                pltpu.make_async_copy(source.at[rows, :], into.at[slot], w_sems.at[slot, which])
+                for which, (source, into) in enumerate(
+                    ((wq_ref, wq_in), (wk_ref, wk_in), (wv_ref, wv_in))
+                )
+            ]
 
         def push(k):
             peer = lax.rem(t + k, n)
             return remote(
-                block(peer), inbox.at[t], send.at[k], recv.at[t], at(d, sec, peer)
+                outbox.at[peer], inbox.at[t], send.at[k], recv.at[t], at(d, sec, peer)
             )
 
-        for k in range(1, n):
-            push(k).start()
-        own.wait()
+        for load in loads(jnp.int32(0)):
+            load.start()
+        for k in range(1, n + 1):
+            owner = lax.rem(t + k, n)
+
+            def project(index, carry):
+                count = (k - 1) * per + index
+
+                @pl.when(count + 1 < n * per)
+                def _():
+                    for load in loads(count + 1):
+                        load.start()
+
+                for load in loads(count):
+                    load.wait()
+                slot = lax.rem(count, 2)
+                value = (
+                    dot_t(gq_ref[...], wq_in[slot])
+                    + dot_t(gkv_ref[:, :kv_cols], wk_in[slot])
+                    + dot_t(gkv_ref[:, kv_cols:], wv_in[slot])
+                ).astype(BF16)
+                columns = pl.ds(pl.multiple_of(index * deep, deep), deep)
+                if k < n:
+                    outbox[owner, :, columns] = value
+                else:
+                    inbox[owner, :, columns] = value
+                return carry
+
+            lax.fori_loop(0, per, project, 0)
+            if k < n:
+                push(k).start()
+
         for k in range(1, n):
             peer = lax.rem(t + k, n)
             remote(
-                block(peer), inbox.at[peer], send.at[k], recv.at[peer], at(d, sec, peer)
+                outbox.at[peer], inbox.at[peer], send.at[k], recv.at[peer], at(d, sec, peer)
             ).wait_recv()
 
         def gather_sum(index, carry):
@@ -385,13 +367,14 @@
             ).wait_send()
 
 
-def finish(n, active, part, x, up, gain, rms):
+def finish(n, active, gq, gkv, x, up, gain, rms, wq, wk, wv):
     many, wide = x.shape
+    deep = 512
     dma = pltpu.SemaphoreType.DMA
     vmem = pl.BlockSpec(memory_space=pltpu.VMEM)
     return pl.pallas_call(
-        functools.partial(finish_body, n, active, part.shape[1]),
-        in_specs=[pl.BlockSpec(memory_space=pl.ANY)] + [vmem] * 4,
+        functools.partial(finish_body, n, active, wq.shape[0]),
+        in_specs=[vmem] * 6 + [pl.BlockSpec(memory_space=pl.ANY)] * 3,
         out_specs=[vmem, vmem],
         out_shape=[
             jax.ShapeDtypeStruct((many, wide), F32),
@@ -399,17 +382,21 @@
         ],
         scratch_shapes=[
             pltpu.VMEM((n, many, wide), BF16),
+            pltpu.VMEM((n, many, wide), BF16),
             pltpu.VMEM((n, many, HD), F32),
-            dma((n,)),
-            dma((n,)),
-            dma((n,)),
-            dma((n,)),
-            dma,
+            pltpu.VMEM((2, deep, wq.shape[1]), BF16),
+            pltpu.VMEM((2, deep, wk.shape[1]), BF16),
+            pltpu.VMEM((2, deep, wv.shape[1]), BF16),
+            dma((2, 3)),
+            dma((n,)),
+            dma((n,)),
+            dma((n,)),
+            dma((n,)),
         ],
         compiler_params=pltpu.CompilerParams(
             collective_id=1 + active, has_side_effects=True, vmem_limit_bytes=BIG
         ),
-    )(part, x, up, gain, rms)
+    )(gq, gkv, x, up, gain, rms, wq, wk, wv)
 
 
 def descend_body(
@@ -543,6 +530,150 @@
     )(g, w)
 
 
+def attend_body(n, active, gather, lens_ref, q_ref, o_ref, kv_ref, cos_ref, sin_ref, *rest):
+    if gather:
+        gq_ref, gkv_ref, kv_out, kv_box, terms, inbox, kv_send, kv_recv, send, recv = rest
+    else:
+        gq_ref, gkv_ref, terms, inbox, send, recv = rest
+        kv_box = kv_ref
+    d, sec, t = lax.axis_index("dp"), lax.axis_index("section"), lax.axis_index("tensor")
+    batch, rows, cols = q_ref.shape
+    kv_cols = kv_box.shape[3] // 2
+    kv_dev = kv_cols // HD
+    group = cols // kv_cols
+    length = n * rows
+    many = rows * group
+    scale = 1.0 / math.sqrt(HD)
+    for k in range(1, n):
+        greet(at(lax.rem(d + k, n), sec, t))
+    pl.semaphore_wait(pltpu.get_barrier_semaphore(), n - 1)
+
+    if gather:
+        for k in range(1, n):
+            remote(
+                kv_ref, kv_box.at[d], kv_send.at[k], kv_recv.at[d],
+                at(lax.rem(d + k, n), sec, t),
+            ).start()
+        kv_box[d] = kv_ref[...]
+        for k in range(1, n):
+            peer = lax.rem(d + k, n)
+            remote(
+                kv_ref, kv_box.at[peer], kv_send.at[k], kv_recv.at[peer], at(peer, sec, t)
+            ).wait_recv()
+        kv_out[...] = kv_box[...]
+
+    @pl.when(sec == active)
+    def _():
+        cosine, sine = cos_ref[...], sin_ref[...]
+
+        def one(index, carry):
+            seq = index // kv_dev
+            kv_head = lax.rem(index, kv_dev)
+            k_lanes = pl.ds(pl.multiple_of(kv_head * HD, HD), HD)
+            v_lanes = pl.ds(pl.multiple_of(kv_cols + kv_head * HD, HD), HD)
+
+            def q_lanes(head):
+                return pl.ds(pl.multiple_of((kv_head * group + head) * HD, HD), HD)
+
+            q_parts, o_parts = [], []
+            for head in range(group):
+                raw = q_ref[seq, :, q_lanes(head)]
+                turned = raw * cosine + pltpu.roll(raw, HD // 2, 1) * sine
+                q_parts.append(turned.astype(BF16))
+                o_parts.append(o_ref[seq, :, q_lanes(head)])
+            q_all = jnp.concatenate(q_parts, 0)
+            o_all = jnp.concatenate(o_parts, 0)
+            keys = jnp.concatenate([kv_box[r, seq, :, k_lanes] for r in range(n)], 0)
+            values = jnp.concatenate([kv_box[r, seq, :, v_lanes] for r in range(n)], 0)
+            row_at = lax.broadcasted_iota(jnp.int32, (many, length), 0) & (rows - 1)
+            query_at = d * rows + row_at
+            key_at = lax.broadcasted_iota(jnp.int32, (many, length), 1)
+            start = length - lens_ref[seq]
+            allowed = (key_at == query_at) | ((key_at < query_at) & (key_at >= start))
+            scores = jnp.where(allowed, dot_t(q_all, keys) * scale, -1e30)
+            highest = jnp.max(scores, -1, keepdims=True)
+            terms_e = jnp.where(allowed, jnp.exp(scores - highest), 0.0)
+            probs = terms_e / jnp.sum(terms_e, -1, keepdims=True)
+            grad_probs = dot_t(o_all, values)
+            row_dot = jnp.sum(probs * grad_probs, -1, keepdims=True)
+            grad_scores = (probs * (grad_probs - row_dot) * scale).astype(BF16)
+            grad_qr = dot_n(grad_scores, keys)
+            grad_k = dot_c(grad_scores, q_all).astype(BF16)
+            grad_v = dot_c(probs.astype(BF16), o_all).astype(BF16)
+            for r in range(n):
+                terms[r, seq, :, k_lanes] = grad_k[r * rows : (r + 1) * rows]
+                terms[r, seq, :, v_lanes] = grad_v[r * rows : (r + 1) * rows]
+            for head in range(group):
+                part = grad_qr[head * rows : (head + 1) * rows]
+                turned = part * cosine - pltpu.roll(part, HD // 2, 1) * sine
+                gq_ref[seq, :, q_lanes(head)] = turned.astype(BF16)
+            return carry
+
+        lax.fori_loop(0, batch * kv_dev, one, 0)
+
+        def push(k):
+            peer = lax.rem(d + k, n)
+            return remote(
+                terms.at[peer], inbox.at[d], send.at[k], recv.at[d], at(peer, sec, t)
+            )
+
+        for k in range(1, n):
+            push(k).start()
+        inbox[d] = terms[d]
+        for k in range(1, n):
+            peer = lax.rem(d + k, n)
+            remote(
+                terms.at[peer], inbox.at[peer], send.at[k], recv.at[peer], at(peer, sec, t)
+            ).wait_recv()
+        for seq in range(batch):
+            total = inbox[0, seq].astype(F32)
+            for r in range(1, n):
+                total = total + inbox[r, seq].astype(F32)
+            for head in range(kv_dev):
+                lanes = slice(head * HD, (head + 1) * HD)
+                part = total[:, lanes]
+                turned = part * cosine - pltpu.roll(part, HD // 2, 1) * sine
+                gkv_ref[seq, :, lanes] = turned.astype(BF16)
+            gkv_ref[seq, :, kv_cols:] = total[:, kv_cols:].astype(BF16)
+        for k in range(1, n):
+            push(k).wait_send()
+
+    if gather:
+        for k in range(1, n):
+            remote(
+                kv_ref, kv_box.at[d], kv_send.at[k], kv_recv.at[d],
+                at(lax.rem(d + k, n), sec, t),
+            ).wait_send()
+
+
+def attend(n, active, gather, lengths, queries, grad_out, kv, cosine, sine):
+    batch, rows, cols = queries.shape
+    both = kv.shape[-1]
+    dma = pltpu.SemaphoreType.DMA
+    vmem = pl.BlockSpec(memory_space=pltpu.VMEM)
+    whole = (n, batch, rows, both)
+    out_shape = [
+        jax.ShapeDtypeStruct((batch, rows, cols), BF16),
+        jax.ShapeDtypeStruct((batch, rows, both), BF16),
+    ]
+    scratch = [pltpu.VMEM(whole, BF16), pltpu.VMEM(whole, BF16)]
+    sems = [dma((n,)), dma((n,))]
+    if gather:
+        out_shape.append(jax.ShapeDtypeStruct(whole, BF16))
+        scratch.append(pltpu.VMEM(whole, BF16))
+        sems = sems + sems
+    return pl.pallas_call(
+        functools.partial(attend_body, n, active, gather),
+        in_specs=[pl.BlockSpec(memory_space=pltpu.SMEM)] + [vmem] * 5,
+        out_specs=[vmem] * len(out_shape),
+        out_shape=out_shape,
+        scratch_shapes=scratch + sems,
+        compiler_params=pltpu.CompilerParams(
+            collective_id=4 + active, has_side_effects=True, vmem_limit_bytes=BIG
+        ),
+    )(lengths, queries, grad_out, kv, cosine, sine)
+
+
 def on_device(
     n_tensor, stored, cotangent, positions, lengths, norm_gain, w_query, w_key, w_value, w_out
 ):
@@ -558,10 +689,6 @@
     section_id = lax.axis_index("section")
     row_ids = dp_id * rows + jnp.arange(rows, dtype=jnp.int32)
     cosine, sine = angle_tables(row_ids.astype(F32))
-    lens = jnp.stack(
-        [lengths, jnp.full_like(lengths, dp_id * rows)], 0
-    )
-
     resp = cotangent.shape[1]
     x_parts, resp_grad = opening(
         n_tensor,
@@ -596,39 +723,44 @@
     kv_own = jnp.concatenate(
         [k_rot.reshape(seqs, rows, kv_cols), values.reshape(seqs, rows, kv_cols)], -1
     ).astype(BF16)
-    kv_all = lax.all_gather(kv_own, "dp", axis=1, tiled=True)
-    k_all, v_all = kv_all[..., :kv_cols], kv_all[..., kv_cols:]
     queries = queries.reshape(seqs, rows, -1)
     gain_own = lax.dynamic_slice_in_dim(gain, tensor_id * width_dev, width_dev, 0)
     x_mine = x_own.reshape(many, width_dev)
     rms_wide = jnp.broadcast_to(inv_rms, (many, HD))
 
-    def backward(active, upstream_own, grad_out):
-        grad_q, key_terms, value_terms = attention_grad(
-            lens, queries, grad_out, k_all, v_all, cosine, sine
-        )
-        kv_sum = lax.psum_scatter(
-            jnp.concatenate([key_terms, value_terms], -1), "dp", scatter_dimension=1, tiled=True
-        ).astype(F32)
-        gk_four = kv_sum[..., :kv_cols].reshape(seqs, rows, -1, HD)
-        grad_k = gk_four * cosine[:, None] - turn_plain(gk_four) * sine[:, None]
-        grad_k = grad_k.astype(BF16).reshape(many, kv_cols)
-        grad_v = kv_sum[..., kv_cols:].astype(BF16).reshape(many, kv_cols)
-        partial = dot_t(grad_q.reshape(many, -1), w_q) + dot_t(grad_k, w_k) + dot_t(grad_v, w_v)
+    def backward(active, upstream_own, grad_q, grad_kv):
         return finish(
             n_tensor,
             active,
-            partial.astype(BF16),
+            grad_q.reshape(many, -1),
+            grad_kv.reshape(many, -1),
             x_mine,
             upstream_own.reshape(many, width_dev),
             gain_own[None],
             rms_wide,
+            w_q,
+            w_k,
+            w_v,
         )
 
-    first, first_low = backward(1, place(cotangent), place(resp_grad))
+    grad_q, grad_kv, kv_all = attend(
+        n_tensor, 1, True, lengths, queries, place(resp_grad), kv_own, cosine, sine
+    )
+    first, first_low = backward(1, place(cotangent), grad_q, grad_kv)
 
     handed, grad_out = descend(n_tensor, first_low, w_o)
-    second, _ = backward(0, handed, grad_out.reshape(seqs, rows, -1))
+    grad_q, grad_kv = attend(
+        n_tensor,
+        0,
+        False,
+        lengths,
+        queries,
+        grad_out.reshape(seqs, rows, -1),
+        kv_all,
+        cosine,
+        sine,
+    )
+    second, _ = backward(0, handed, grad_q, grad_kv)
     result = jnp.where(section_id == 0, second, first)
     return result.reshape(1, seqs, rows, width_dev)
 

time: 341 us -> 247 us (0.72)
  matrix products: 66.9 us -> 20.2 us
  waiting for transfers between devices: 19.7 us -> 0 us
  blocking collectives: 13.9 us -> 0 us
  between operations: 13.8 us -> 0.22 us
  Pallas kernels: 207 us -> 214 us
  other arithmetic: 13 us -> 7.98 us
    dot_general x6 -> x0, matrix products: 50.8 us -> none  [dot_t(): lax.dot_general(left, right, (((1,), (1,)), ((), ())), preferred_element_...]
    pallas_call x4, Pallas kernels: 54.1 us -> 80 us  [the longest x2 52.2 us: finish(): pl.pallas_call(functools.partial(finish_body, n, active, wq.shape[0]), in...]
    reduce_scatter x2 -> x0, waiting for transfers between devices: 19.7 us -> none  [backward(): lax.psum_scatter(jnp.concatenate([key_terms, value_terms], -1), 'dp', sca...]
    all_gather x1 -> x0, blocking collectives: 13.9 us -> none  [on_device(): kv_all = lax.all_gather(kv_own, 'dp', axis=1, tiled=True)]
    pallas_call x1, Pallas kernels: 83.6 us -> 73.5 us  [descend(): pl.pallas_call(functools.partial(descend_body, n), in_specs=[vmem, pl.Blo...]
    pallas_call x1, Pallas kernels: 69.7 us -> 60.6 us  [opening(): pl.pallas_call(functools.partial(opening_body, n), in_specs=[pl.BlockSpec...]
  transfers between devices with their start and end apart: 2 -> 0, of which waited for: 2 -> 0; matrix products, arithmetic and copies ran while one was open for 11% -> 0% of each run, Pallas kernels for 0% -> 0%
where the time goes in v3:
time: 247 us; the launch traced here: 246 us
  Pallas kernels  214 us (87%)
  matrix products  20.2 us (8%)
  other arithmetic  7.98 us (3%)
  local copies, waits for them, and re-layouts  3.97 us (2%)
    pallas_call x1, Pallas kernels, descend(): pl.pallas_call(functools.partial(descend_body, n), in_specs=[vmem, pl.Blo...  73.5 us
    pallas_call x1, Pallas kernels, opening(): pl.pallas_call(functools.partial(opening_body, n), in_specs=[pl.BlockSpec...  60.6 us
    pallas_call x2, Pallas kernels, finish(): pl.pallas_call(functools.partial(finish_body, n, active, wq.shape[0]), in...  52.2 us
    pallas_call x2, Pallas kernels, attend(): pl.pallas_call(functools.partial(attend_body, n, active, gather), in_spec...  27.8 us
    dot_general x3, matrix products, dot_n(): lax.dot_general(left, right, (((1,), (0,)), ((), ())), preferred_element_...  17.7 us

profile of v3, /device:TPU:0, one launch (start us, length us, event | category | flops | bytes accessed | tf_op | source)
XLA Modules:
  0.0 246.4 jit_solution(12794021670803234054)
XLA Ops:
  0.0 1.4 constant_dynamic-slice_fusion
  1.4 60.6 %shard_map.91 = (bf16[4,128,2048]{2,1,0:T(8,128)(2,1)}, bf16[64,2048]{1,0:T(8,128)(2,1)}) custom-call(bf16[128,2048]{1,0:T(8,128)(2,1)} %bitcast.57, bf16[64,2048]{1,0:T(8,128)(2,1)} %bitcast.63, bf16[2048,2048]{1,0:T(8,128)(2,1)} %bitcast.51), custom_call_target="tpu_custom_call" | custom-call | tf_op jit(solution)/shard_map/pallas_call | solution.py:216
  61.9 0.0 copy-start
  61.9 2.2 multiply_reduce_fusion
  64.2 2.1 fusion.7
  66.3 0.0 copy-done
  66.4 0.0 copy-start.1
  66.4 0.8 fusion.15
  67.1 1.4 copy-done.1
  68.5 0.8 fusion.17
  69.3 0.0 copy-start.6
  69.3 0.0 copy-start.7
  69.3 16.2 %fusion.19 = f32[128,2048]{1,0:T(8,128)} fusion(bf16[1,8192,2048]{2,1,0:T(8,128)(2,1)} %param.14, bf16[128,2048]{1,0:T(8,128)(2,1)S(1)} %get-tuple-element.38, bf16[128,2048]{1,0:T(8,128)(2,1)S(1)} %get-tuple-element.37, bf16[128,2048]{1,0:T(8,128)(2,1)S(1)} %get-tuple-element.36, bf16[128,2048]{1,0:T(8,128)(2,1)S(1)} %get-tuple-element.35), kind=kOutput, calls=%fused_computation.41 | convolution fusion | flops 4303355904 | bytes 36700160 | tf_op jit(solution)/shard_map/dot_general | solution.py:23
  85.6 0.0 copy-start.2
  85.6 0.1 reshape.93
  85.6 0.2 fusion.22
  85.8 0.2 pad_maximum_fusion.1
  86.0 0.1 concatenate.21
  86.2 0.2 multiply_cosine_fusion
  86.4 0.1 pad_maximum_fusion.4.sin_ref
  86.5 0.0 copy-start.4
  86.5 0.1 pad_maximum_fusion.3.cos_ref
  86.6 0.0 copy-start.5
  86.7 0.7 pad_maximum_fusion.2.kv_ref
  87.4 0.0 copy-done.6
  87.4 0.0 copy-done.7
  87.4 1.2 convolution_convert_fusion.1.o_ref
  88.6 0.0 copy-done.4
  88.6 0.0 copy-done.5
  88.6 12.5 %shard_map.92 = (bf16[2,64,2048]{2,1,0:T(8,128)(2,1)}, bf16[2,64,512]{2,1,0:T(8,128)(2,1)}, bf16[4,2,64,512]{3,2,1,0:T(8,128)(2,1)}) custom-call(s32[2]{0:T(128)} %lens_ref.3, f32[2,64,2048]{2,1,0:T(8,128)} %bitcast.60, bf16[2,64,2048]{2,1,0:T(8,128)(2,1)} %convolution_convert_fusion.1.o_ref, bf16[2,64,512]{2,1,0:T(8,128)(2,1)} %pad_maximum_fusion.2.kv_ref, ...), custom_call_target="tpu_custom_call" | custom-call | tf_op jit(solution)/shard_map/pallas_call | solution.py:665
  101.1 0.7 broadcast_in_dim.2.rms_ref
  101.8 0.0 copy-done.2
  101.8 1.2 convolution_convert_fusion
  103.0 4.1 %shard_map.93 = (f32[128,2048]{1,0:T(8,128)}, bf16[128,2048]{1,0:T(8,128)(2,1)}) custom-call(bf16[128,2048]{1,0:T(8,128)(2,1)} %bitcast.65, bf16[128,512]{1,0:T(8,128)(2,1)} %bitcast.74, bf16[128,2048]{1,0:T(8,128)(2,1)} %bitcast.58, bf16[128,2048]{1,0:T(8,128)(2,1)} %bitcast.62, f32[1,2048]{1,0:T(1,128)} %get-tuple-element.41.gain_ref, ...), custom_call_target="tpu_custom_call" | custom-call | tf_op jit(solution)/shard_map/pallas_call | solution.py:375
  107.2 73.5 %shard_map.94 = (bf16[128,2048]{1,0:T(8,128)(2,1)}, bf16[128,2048]{1,0:T(8,128)(2,1)}) custom-call(bf16[128,2048]{1,0:T(8,128)(2,1)} %get-tuple-element.27.g_ref, bf16[2048,2048]{1,0:T(8,128)(2,1)} %bitcast.52), custom_call_target="tpu_custom_call" | custom-call | tf_op jit(solution)/shard_map/pallas_call | solution.py:504
  180.7 15.3 %shard_map.95 = (bf16[2,64,2048]{2,1,0:T(8,128)(2,1)}, bf16[2,64,512]{2,1,0:T(8,128)(2,1)}) custom-call(s32[2]{0:T(128)} %lens_ref.3, f32[2,64,2048]{2,1,0:T(8,128)} %bitcast.61, bf16[2,64,2048]{2,1,0:T(8,128)(2,1)} %bitcast.66, bf16[4,2,64,512]{3,2,1,0:T(8,128)(2,1)} %get-tuple-element.29.kv_ref, f32[64,128]{1,0:T(8,128)} %copy-done.5, f32[64,128]{1,0:T(8,128)} %copy-done.4), custom_call_target="tpu_custom_call" | custom-call | tf_op jit(solution)/shard_map/pallas_call | solution.py:665
  196.0 0.0 copy-start.3
  196.0 48.1 %shard_map.96 = (f32[128,2048]{1,0:T(8,128)}, bf16[128,2048]{1,0:T(8,128)(2,1)}) custom-call(bf16[128,2048]{1,0:T(8,128)(2,1)} %bitcast.64, bf16[128,512]{1,0:T(8,128)(2,1)} %bitcast.73, bf16[128,2048]{1,0:T(8,128)(2,1)} %bitcast.59, bf16[128,2048]{1,0:T(8,128)(2,1)} %get-tuple-element.32.up_ref, f32[1,2048]{1,0:T(1,128)} %get-tuple-element.41.gain_ref, ...), custom_call_target="tpu_custom_call" | custom-call | tf_op jit(solution)/shard_map/pallas_call | solution.py:375
  244.1 0.0 copy-done.3
  244.1 2.3 broadcast_select_fusion
  (8 shorter events, 0.1 us)
Async XLA Ops:
  61.9 4.4 %copy-start = (bf16[1,8192,256]{2,1,0:T(8,128)(2,1)S(1)}, bf16[1,8192,256]{2,1,0:T(8,128)(2,1)}, u32[]{:S(2)}) copy-start(bf16[1,8192,256]{2,1,0:T(8,128)(2,1)} %param.16) | copy-start | bytes 12582916
  66.4 2.2 copy-start.1
  69.3 18.0 %copy-start.6 = (bf16[64,2048]{1,0:T(8,128)(2,1)S(1)}, bf16[64,2048]{1,0:T(8,128)(2,1)}, u32[]{:S(2)}) copy-start(bf16[64,2048]{1,0:T(8,128)(2,1)} %get-tuple-element.22) | copy-start | bytes 786436
  69.3 18.0 %copy-start.7 = (s32[2,32]{1,0:T(2,128)S(1)}, s32[2,32]{1,0:T(2,128)}, u32[]{:S(2)}) copy-start(s32[2,32]{1,0:T(2,128)} %param.11) | copy-start | bytes 772
  85.6 16.2 %copy-start.2 = (bf16[2,32,2048]{2,1,0:T(8,128)(2,1)S(1)}, bf16[2,32,2048]{2,1,0:T(8,128)(2,1)}, u32[]{:S(2)}) copy-start(bf16[2,32,2048]{2,1,0:T(8,128)(2,1)} %param.10) | copy-start | bytes 786436
  86.5 2.1 copy-start.4
  86.6 2.0 copy-start.5
  196.0 48.1 %copy-start.3 = (f32[128,2048]{1,0:T(8,128)S(1)}, f32[128,2048]{1,0:T(8,128)}, u32[]{:S(2)}) copy-start(f32[128,2048]{1,0:T(8,128)} %get-tuple-element.34) | copy-start | bytes 3145732

commit v4 on v3

--- a/solution.py
+++ b/solution.py
@@ -79,11 +79,18 @@
 
 
 def opening_body(
-    n, x_ref, cot_ref, w_ref, x_out, resp_out, cot_in, w_in, part, inbox,
-    x_send, x_recv, cot_sems, w_sem, part_send, part_recv, own_sem, turn_sem,
+    n, width, x_ref, cot_ref, w_ref, gain_ref, wq_ref, wk_ref, wv_ref,
+    q_out, kv_out, rms_out, resp_out,
+    x_box, cot_in, w_in, part, inbox, wq_in, wk_in, wv_in,
+    x_send, x_recv, cot_sems, w_sem, part_send, part_recv, own_sem, tile_sems, turn_sem,
 ):
     d, sec, t = lax.axis_index("dp"), lax.axis_index("section"), lax.axis_index("tensor")
+    many, wide = x_ref.shape
+    kv_cols = wk_in.shape[2]
+    deep = wq_in.shape[1]
+    per = wide // deep
     crossing = jnp.where(d == t, 0, 1)
+    onward = jnp.where(2 * t >= n, n - 1, 1)
     for k in range(1, n):
         greet(at(d, sec, lax.rem(t + k, n)))
         greet(at(lax.rem(d + k, n), sec, t))
@@ -95,35 +102,42 @@
 
     pl.semaphore_wait(pltpu.get_barrier_semaphore(), 2 * n - 1 + crossing)
 
-    own = pltpu.make_async_copy(x_ref, x_out.at[t], own_sem)
+    own = pltpu.make_async_copy(x_ref, x_box.at[t], own_sem)
     own.start()
+
+    def loads(count):
+        owner = lax.rem(t + (count // per) * onward, n)
+        rows = pl.ds(pl.multiple_of(owner * wide + lax.rem(count, per) * deep, deep), deep)
+        slot = lax.rem(count, 2)
+        return [
+            pltpu.make_async_copy(source.at[rows, :], into.at[slot], tile_sems.at[slot, which])
+            for which, (source, into) in enumerate(
+                ((wq_ref, wq_in), (wk_ref, wk_in), (wv_ref, wv_in))
+            )
+        ]
+
+    for load in loads(jnp.int32(0)):
+        load.start()
 
     @pl.when(sec == 0)
     def _():
         pl.semaphore_wait(turn_sem, 1)
 
-    def pass_on(src, slot, right):
-        step = 1 if right else -1
+    def spread(k):
         return remote(
-            src, x_out.at[slot], x_send.at[slot, int(right)], x_recv.at[slot],
-            at(d, sec, t + step),
+            x_ref, x_box.at[t], x_send.at[k], x_recv.at[t], at(d, sec, lax.rem(t + k, n))
         )
 
-    @pl.when(t + 1 < n)
-    def _():
-        pass_on(x_ref, t, True).start()
-
-    @pl.when(t > 0)
-    def _():
-        pass_on(x_ref, t, False).start()
-
-    load = pltpu.make_async_copy(w_ref, w_in, w_sem)
+    for k in range(1, n):
+        spread(k).start()
+
+    w_load = pltpu.make_async_copy(w_ref, w_in, w_sem)
     swap = remote(cot_ref, cot_in, cot_sems.at[0], cot_sems.at[1], at(t, sec, d))
     keep = pltpu.make_async_copy(cot_ref, cot_in, cot_sems.at[2])
 
     @pl.when(sec == 1)
     def _():
-        load.start()
+        w_load.start()
 
         @pl.when(d != t)
         def _():
@@ -132,6 +146,11 @@
         @pl.when(d == t)
         def _():
             keep.start()
+
+    def give(k):
+        return remote(
+            part, inbox.at[d], part_send.at[k], part_recv.at[d], at(lax.rem(d + k, n), sec, t)
+        )
 
     def respond():
         @pl.when(d != t)
@@ -142,106 +161,129 @@
         def _():
             keep.wait()
 
-        load.wait()
+        w_load.wait()
 
         def store(start, size, value):
             part[:, pl.ds(start, size)] = value
 
         tiled_dot_t(cot_in, w_in, store)
         for k in range(1, n):
-            remote(
-                part, inbox.at[d], part_send.at[k], part_recv.at[d],
-                at(lax.rem(d + k, n), sec, t),
-            ).start()
-
-    for k in range(1, n):
-        left, right = t - k, t + k
-
-        @pl.when(left >= 0)
-        def _():
-            pass_on(x_ref, left, True).wait_recv()
-
-            @pl.when(t + 1 < n)
+            give(k).start()
+
+    q_out[...] = jnp.zeros_like(q_out)
+    kv_out[...] = jnp.zeros_like(kv_out)
+    rms_out[...] = jnp.zeros_like(rms_out)
+    own.wait()
+    for step in range(n):
+        owner = lax.rem(t + step * onward, n)
+        if step:
+            remote(
+                x_ref, x_box.at[owner], x_send.at[step], x_recv.at[owner], at(d, sec, owner)
+            ).wait_recv()
+        if step == n - 1:
+
+            @pl.when(sec == 1)
             def _():
-                pass_on(x_out.at[left], left, True).start()
-
-        @pl.when(right < n)
-        def _():
-            pass_on(x_ref, right, False).wait_recv()
-
-            @pl.when(t > 0)
+                pl.semaphore_signal(
+                    turn_sem, inc=1, device_id=at(d, 0, t), device_id_type=MESH
+                )
+
+        def project(index, carry):
+            count = step * per + index
+
+            @pl.when(count + 1 < n * per)
             def _():
-                pass_on(x_out.at[right], right, False).start()
-
-        if k == 1:
+                for load in loads(count + 1):
+                    load.start()
+
+            columns = pl.ds(pl.multiple_of(index * deep, deep), deep)
+            piece = x_box[owner, :, columns].astype(F32)
+            squares = jnp.sum(piece * piece, -1, keepdims=True)
+            rms_out[...] += jnp.broadcast_to(squares, (many, HD))
+            scaled = (piece * gain_ref[owner, :, columns]).astype(BF16)
+            for load in loads(count):
+                load.wait()
+            slot = lax.rem(count, 2)
+            q_out[...] += dot_n(scaled, wq_in[slot])
+            kv_out[:, :kv_cols] += dot_n(scaled, wk_in[slot])
+            kv_out[:, kv_cols:] += dot_n(scaled, wv_in[slot])
+            return carry
+
+        lax.fori_loop(0, per, project, 0)
+        if step == 0:
             pl.when(sec == 1)(respond)
 
-    own.wait()
+    tile = 16
+
+    def settle(index, carry):
+        rows = pl.ds(pl.multiple_of(index * tile, tile), tile)
+        rms = lax.rsqrt(rms_out[rows, :] / width + EPS)
+        rms_out[rows, :] = rms
+        q_out[rows, :] = q_out[rows, :] * rms[:, :1]
+        kv_out[rows, :] = kv_out[rows, :] * rms[:, :1]
+        return carry
+
+    lax.fori_loop(0, many // tile, settle, 0)
 
     @pl.when(sec == 1)
     def _():
-        pl.semaphore_signal(turn_sem, inc=1, device_id=at(d, 0, t), device_id_type=MESH)
         total = part[...].astype(F32)
         for k in range(1, n):
             peer = lax.rem(d + k, n)
-            move = remote(
+            remote(
                 part, inbox.at[peer], part_send.at[k], part_recv.at[peer], at(peer, sec, t)
-            )
-            move.wait_recv()
+            ).wait_recv()
             total = total + inbox[peer].astype(F32)
         resp_out[...] = total.astype(BF16)
         for k in range(1, n):
-            peer = lax.rem(d + k, n)
-            remote(
-                part, inbox.at[d], part_send.at[k], part_recv.at[d], at(peer, sec, t)
-            ).wait_send()
-
-    for k in range(n):
-        left, right = t - k, t + k
-
-        @pl.when((left >= 0) & (t + 1 < n))
-        def _():
-            pass_on(x_ref, left, True).wait_send()
-
-        @pl.when((right < n) & (t > 0))
-        def _():
-            pass_on(x_ref, right, False).wait_send()
-
-
-def opening(n, x, cot, w):
+            give(k).wait_send()
+
+    for k in range(1, n):
+        spread(k).wait_send()
+
+
+def opening(n, x, cot, w, gain, wq, wk, wv):
     many, wide = x.shape
     resp = cot.shape[0]
     cols = w.shape[0]
+    kv_cols = wk.shape[1]
+    deep = 512
     dma = pltpu.SemaphoreType.DMA
+    vmem = pl.BlockSpec(memory_space=pltpu.VMEM)
+    hbm = pl.BlockSpec(memory_space=pl.ANY)
     return pl.pallas_call(
-        functools.partial(opening_body, n),
-        in_specs=[pl.BlockSpec(memory_space=pl.ANY)] * 3,
-        out_specs=[
-            pl.BlockSpec(memory_space=pl.ANY),
-            pl.BlockSpec(memory_space=pltpu.VMEM),
-        ],
+        functools.partial(opening_body, n, wq.shape[0]),
+        in_specs=[hbm, hbm, hbm, vmem, hbm, hbm, hbm],
+        out_specs=[vmem] * 4,
         out_shape=[
-            jax.ShapeDtypeStruct((n, many, wide), BF16),
+            jax.ShapeDtypeStruct((many, cols), F32),
+            jax.ShapeDtypeStruct((many, 2 * kv_cols), F32),
+            jax.ShapeDtypeStruct((many, HD), F32),
             jax.ShapeDtypeStruct((resp, cols), BF16),
         ],
         scratch_shapes=[
+            pltpu.VMEM((n, many, wide), BF16),
             pltpu.VMEM((resp, wide), BF16),
             pltpu.VMEM(w.shape, BF16),
             pltpu.VMEM((resp, cols), BF16),
             pltpu.VMEM((n, resp, cols), BF16),
-            dma((n, 2)),
+            pltpu.VMEM((2, deep, cols), BF16),
+            pltpu.VMEM((2, deep, kv_cols), BF16),
+            pltpu.VMEM((2, deep, kv_cols), BF16),
+            dma((n,)),
             dma((n,)),
             dma((3,)),
             dma,
             dma((n,)),
             dma((n,)),
             dma,
+            dma((2, 3)),
             pltpu.SemaphoreType.REGULAR,
         ],
         compiler_params=pltpu.CompilerParams(
             collective_id=0, has_side_effects=True, vmem_limit_bytes=BIG
         ),
-    )(x, cot, w)
+    )(x, cot, w, gain.reshape(n, 1, wide), wq, wk, wv)
 
 
 def finish_body(
@@ -273,10 +315,15 @@
                 )
             ]
 
-        def push(k):
+        def push(k, index):
             peer = lax.rem(t + k, n)
+            columns = pl.ds(pl.multiple_of(index * deep, deep), deep)
             return remote(
-                outbox.at[peer], inbox.at[t], send.at[k], recv.at[t], at(d, sec, peer)
+                outbox.at[peer, :, columns],
+                inbox.at[t, :, columns],
+                send.at[k, index],
+                recv.at[t, index],
+                at(d, sec, peer),
             )
 
         for load in loads(jnp.int32(0)):
@@ -303,19 +350,24 @@
                 columns = pl.ds(pl.multiple_of(index * deep, deep), deep)
                 if k < n:
                     outbox[owner, :, columns] = value
+                    push(k, index).start()
                 else:
                     inbox[owner, :, columns] = value
                 return carry
 
             lax.fori_loop(0, per, project, 0)
-            if k < n:
-                push(k).start()
 
         for k in range(1, n):
             peer = lax.rem(t + k, n)
-            remote(
-                outbox.at[peer], inbox.at[peer], send.at[k], recv.at[peer], at(d, sec, peer)
-            ).wait_recv()
+            for index in range(per):
+                columns = pl.ds(index * deep, deep)
+                remote(
+                    outbox.at[peer, :, columns],
+                    inbox.at[peer, :, columns],
+                    send.at[k, index],
+                    recv.at[peer, index],
+                    at(d, sec, peer),
+                ).wait_recv()
 
         def gather_sum(index, carry):
             rows = pl.ds(pl.multiple_of(index * tile, tile), tile)
@@ -360,7 +412,8 @@
 
         lax.fori_loop(0, many // tile, settle, 0)
         for k in range(1, n):
-            push(k).wait_send()
+            for index in range(per):
+                push(k, index).wait_send()
             peer = lax.rem(t + k, n)
             remote(
                 stats.at[t], stats.at[t], stat_send.at[k], stat_recv.at[t], at(d, sec, peer)
@@ -388,8 +441,8 @@
             pltpu.VMEM((2, deep, wk.shape[1]), BF16),
             pltpu.VMEM((2, deep, wv.shape[1]), BF16),
             dma((2, 3)),
-            dma((n,)),
-            dma((n,)),
+            dma((n, wide // deep)),
+            dma((n, wide // deep)),
             dma((n,)),
             dma((n,)),
         ],
@@ -690,11 +743,15 @@
     row_ids = dp_id * rows + jnp.arange(rows, dtype=jnp.int32)
     cosine, sine = angle_tables(row_ids.astype(F32))
     resp = cotangent.shape[1]
-    x_parts, resp_grad = opening(
+    queries, key_values, rms_wide, resp_grad = opening(
         n_tensor,
         x_own.reshape(many, width_dev),
         cotangent.reshape(seqs * resp, width_dev),
         w_o,
+        gain,
+        w_q,
+        w_k,
+        w_v,
     )
     resp_grad = resp_grad.reshape(seqs, resp, -1)
     placed = (positions[:, None, :] == row_ids[None, :, None]).astype(BF16)
@@ -702,22 +759,7 @@
     def place(small):
         return jnp.einsum("spr,srd->spd", placed, small, preferred_element_type=F32).astype(BF16)
 
-    squares = jnp.sum(jnp.square(x_parts.astype(F32)), (0, 2))[:, None]
-    inv_rms = lax.rsqrt(squares / width + EPS)
-    normed = jnp.concatenate(
-        [
-            (
-                x_parts[part].astype(F32)
-                * inv_rms
-                * gain[part * width_dev : (part + 1) * width_dev]
-            ).astype(BF16)
-            for part in range(n_tensor)
-        ],
-        1,
-    )
-    queries, keys, values = lax.optimization_barrier(
-        (dot_n(normed, w_q), dot_n(normed, w_k), dot_n(normed, w_v))
-    )
+    keys, values = key_values[:, :kv_cols], key_values[:, kv_cols:]
     k_four = keys.reshape(seqs, rows, -1, HD)
     k_rot = k_four * cosine[:, None] + turn_plain(k_four) * sine[:, None]
     kv_own = jnp.concatenate(
@@ -726,7 +768,6 @@
     queries = queries.reshape(seqs, rows, -1)
     gain_own = lax.dynamic_slice_in_dim(gain, tensor_id * width_dev, width_dev, 0)
     x_mine = x_own.reshape(many, width_dev)
-    rms_wide = jnp.broadcast_to(inv_rms, (many, HD))
 
     def backward(active, upstream_own, grad_q, grad_kv):
         return finish(

time: 247 us -> 240 us (0.972)
  matrix products: 20.2 us -> 4.36 us
  Pallas kernels: 214 us -> 227 us
  other arithmetic: 7.98 us -> 3.6 us
    dot_general x3 -> x0, matrix products: 17.7 us -> none  [dot_n(): lax.dot_general(left, right, (((1,), (0,)), ((), ())), preferred_element_...]
    pallas_call x1, Pallas kernels: 60.6 us -> 74.7 us  [opening(): pl.pallas_call(functools.partial(opening_body, n, wq.shape[0]), in_specs=...]
    pallas_call x1, Pallas kernels: 73.5 us -> 62.8 us  [descend(): pl.pallas_call(functools.partial(descend_body, n), in_specs=[vmem, pl.Blo...]
    pallas_call x2, Pallas kernels: 52.2 us -> 58.9 us  [finish(): pl.pallas_call(functools.partial(finish_body, n, active, wq.shape[0]), in...]
    pallas_call x2, Pallas kernels: 27.8 us -> 30.9 us  [attend(): pl.pallas_call(functools.partial(attend_body, n, active, gather), in_spec...]
where the time goes in v4:
time: 240 us; the launch traced here: 239 us
  Pallas kernels  227 us (95%)
  matrix products  4.36 us (2%)
  other arithmetic  3.6 us (2%)
  local copies, waits for them, and re-layouts  3.58 us (1%)
    pallas_call x1, Pallas kernels, opening(): pl.pallas_call(functools.partial(opening_body, n, wq.shape[0]), in_specs=...  74.7 us
    pallas_call x1, Pallas kernels, descend(): pl.pallas_call(functools.partial(descend_body, n), in_specs=[vmem, pl.Blo...  62.8 us
    pallas_call x2, Pallas kernels, finish(): pl.pallas_call(functools.partial(finish_body, n, active, wq.shape[0]), in...  58.9 us
    pallas_call x2, Pallas kernels, attend(): pl.pallas_call(functools.partial(attend_body, n, active, gather), in_spec...  30.9 us

profile of v4, /device:TPU:0, one launch (start us, length us, event | category | flops | bytes accessed | tf_op | source)
XLA Modules:
  0.0 239.0 jit_solution(16457417661630500291)
XLA Ops:
  0.0 1.3 constant_dynamic-slice_fusion.gain_ref
  1.3 0.2 multiply_cosine_fusion
  1.5 0.1 pad_maximum_fusion.2.cos_ref
  1.6 0.0 copy-start.1
  1.6 0.1 pad_maximum_fusion.3.sin_ref
  1.7 0.0 copy-start.2
  1.8 2.2 convolution_convert_fusion
  4.0 0.0 copy-start.3
  4.0 74.7 %shard_map.91 = (f32[128,2048]{1,0:T(8,128)}, f32[128,512]{1,0:T(8,128)}, f32[128,128]{1,0:T(8,128)}, bf16[64,2048]{1,0:T(8,128)(2,1)}) custom-call(bf16[128,2048]{1,0:T(8,128)(2,1)} %bitcast.39, bf16[64,2048]{1,0:T(8,128)(2,1)} %bitcast.46, bf16[2048,2048]{1,0:T(8,128)(2,1)} %bitcast.37, f32[4,1,2048]{2,1,0:T(1,128)} %bitcast.58, ...), custom_call_target="tpu_custom_call" | custom-call | tf_op jit(solution)/shard_map/pallas_call | solution.py:254
  78.6 0.0 copy-done.1
  78.7 0.0 copy-done.2
  78.7 0.9 slice.21
  79.6 0.9 slice.13
  80.5 0.1 reshape.69
  80.6 0.2 fusion.8
  80.8 0.2 pad_maximum_fusion
  81.0 0.1 concatenate.17
  81.1 0.7 pad_maximum_fusion.1.kv_ref
  81.8 0.0 copy-done.3
  81.8 2.2 convolution_convert_fusion.1.o_ref
  84.0 15.7 %shard_map.92 = (bf16[2,64,2048]{2,1,0:T(8,128)(2,1)}, bf16[2,64,512]{2,1,0:T(8,128)(2,1)}, bf16[4,2,64,512]{3,2,1,0:T(8,128)(2,1)}) custom-call(s32[2]{0:T(128)} %lens_ref.3, f32[2,64,2048]{2,1,0:T(8,128)} %bitcast.42, bf16[2,64,2048]{2,1,0:T(8,128)(2,1)} %convolution_convert_fusion.1.o_ref, bf16[2,64,512]{2,1,0:T(8,128)(2,1)} %pad_maximum_fusion.1.kv_ref, ...), custom_call_target="tpu_custom_call" | custom-call | tf_op jit(solution)/shard_map/pallas_call | solution.py:718
  99.6 13.9 %shard_map.93 = (f32[128,2048]{1,0:T(8,128)}, bf16[128,2048]{1,0:T(8,128)(2,1)}) custom-call(bf16[128,2048]{1,0:T(8,128)(2,1)} %bitcast.48, bf16[128,512]{1,0:T(8,128)(2,1)} %bitcast.57, bf16[128,2048]{1,0:T(8,128)(2,1)} %bitcast.40, bf16[128,2048]{1,0:T(8,128)(2,1)} %bitcast.44, f32[1,2048]{1,0:T(1,128)} %constant_dynamic-slice_fusion.gain_ref, ...), custom_call_target="tpu_custom_call" | custom-call | tf_op jit(solution)/shard_map/pallas_call | solution.py:428
  113.6 62.8 %shard_map.94 = (bf16[128,2048]{1,0:T(8,128)(2,1)}, bf16[128,2048]{1,0:T(8,128)(2,1)}) custom-call(bf16[128,2048]{1,0:T(8,128)(2,1)} %get-tuple-element.25.g_ref, bf16[2048,2048]{1,0:T(8,128)(2,1)} %bitcast.38), custom_call_target="tpu_custom_call" | custom-call | tf_op jit(solution)/shard_map/pallas_call | solution.py:557
  176.4 15.3 %shard_map.95 = (bf16[2,64,2048]{2,1,0:T(8,128)(2,1)}, bf16[2,64,512]{2,1,0:T(8,128)(2,1)}) custom-call(s32[2]{0:T(128)} %lens_ref.3, f32[2,64,2048]{2,1,0:T(8,128)} %bitcast.43, bf16[2,64,2048]{2,1,0:T(8,128)(2,1)} %bitcast.49, bf16[4,2,64,512]{3,2,1,0:T(8,128)(2,1)} %get-tuple-element.27.kv_ref, f32[64,128]{1,0:T(8,128)} %copy-done.1, f32[64,128]{1,0:T(8,128)} %copy-done.2), custom_call_target="tpu_custom_call" | custom-call | tf_op jit(solution)/shard_map/pallas_call | solution.py:718
  191.7 0.0 copy-start
  191.7 45.0 %shard_map.96 = (f32[128,2048]{1,0:T(8,128)}, bf16[128,2048]{1,0:T(8,128)(2,1)}) custom-call(bf16[128,2048]{1,0:T(8,128)(2,1)} %bitcast.47, bf16[128,512]{1,0:T(8,128)(2,1)} %bitcast.56, bf16[128,2048]{1,0:T(8,128)(2,1)} %bitcast.41, bf16[128,2048]{1,0:T(8,128)(2,1)} %get-tuple-element.30.up_ref, f32[1,2048]{1,0:T(1,128)} %constant_dynamic-slice_fusion.gain_ref, ...), custom_call_target="tpu_custom_call" | custom-call | tf_op jit(solution)/shard_map/pallas_call | solution.py:428
  236.7 0.0 copy-done
  236.7 2.3 broadcast_select_fusion
  (7 shorter events, 0.1 us)
Async XLA Ops:
  1.6 77.1 %copy-start.1 = (f32[64,128]{1,0:T(8,128)}, f32[64,128]{1,0:T(8,128)S(1)}, u32[]{:S(2)}) copy-start(f32[64,128]{1,0:T(8,128)S(1)} %pad_maximum_fusion.2.cos_ref) | copy-start | bytes 98308
  1.7 77.0 %copy-start.2 = (f32[64,128]{1,0:T(8,128)}, f32[64,128]{1,0:T(8,128)S(1)}, u32[]{:S(2)}) copy-start(f32[64,128]{1,0:T(8,128)S(1)} %pad_maximum_fusion.3.sin_ref) | copy-start | bytes 98308
  4.0 77.8 %copy-start.3 = (s32[2,32]{1,0:T(2,128)S(1)}, s32[2,32]{1,0:T(2,128)}, u32[]{:S(2)}) copy-start(s32[2,32]{1,0:T(2,128)} %param.11) | copy-start | bytes 772
  191.7 45.0 %copy-start = (f32[128,2048]{1,0:T(8,128)S(1)}, f32[128,2048]{1,0:T(8,128)}, u32[]{:S(2)}) copy-start(f32[128,2048]{1,0:T(8,128)} %get-tuple-element.32) | copy-start | bytes 3145732

commit v5 on v4

--- a/solution.py
+++ b/solution.py
@@ -489,19 +489,29 @@
                 mid.at[slot], mid.at[slot], g_send.at[0], g_recv.at[slot], at(d, 1, slot)
             ).wait_recv()
 
-        def move(k):
-            peer = lax.rem(d + k, n)
+        onward = jnp.where(2 * t >= n, n - 1, 1)
+
+        def move(slot):
             return remote(
-                mid.at[peer], spread.at[d], s_send.at[k], s_recv.at[d], at(peer, 0, t)
+                mid.at[slot], spread.at[d], s_send.at[slot], s_recv.at[d], at(slot, 0, t)
             )
 
-        for k in range(1, n):
-            arrived(lax.rem(d + k, n))
-            move(k).start()
-        arrived(d)
+        for step in range(n):
+            slot = lax.rem(t + step * onward, n)
+            arrived(slot)
+
+            @pl.when(slot != d)
+            def _():
+                move(slot).start()
+
         keep = pltpu.make_async_copy(mid.at[t], up_out, up_sem)
         keep.start()
         load.wait()
+
+        def store_own(start, size, value):
+            outbox[d, :, pl.ds(start, size)] = value
+
+        tiled_dot_t(mid.at[d], w_in, store_own)
 
         def give(k):
             peer = lax.rem(d + k, n)
@@ -522,10 +532,6 @@
             tiled_dot_t(spread.at[peer], w_in, store)
             give(k).start()
 
-        def store_own(start, size, value):
-            outbox[d, :, pl.ds(start, size)] = value
-
-        tiled_dot_t(mid.at[d], w_in, store_own)
         for k in range(1, n):
             peer = lax.rem(d + k, n)
             remote(
@@ -545,7 +551,7 @@
         lax.fori_loop(0, go_out.shape[0] // tile, add, 0)
         keep.wait()
         for k in range(1, n):
-            move(k).wait_send()
+            move(lax.rem(d + k, n)).wait_send()
             give(k).wait_send()
 
 

time: 240 us -> 241 us (level)
    pallas_call x2, Pallas kernels: 30.9 us -> 33.4 us  [attend(): pl.pallas_call(functools.partial(attend_body, n, active, gather), in_spec...]
where the time goes in v5:
time: 241 us; the launch traced here: 240 us
  Pallas kernels  228 us (95%)
  matrix products  4.36 us (2%)
  other arithmetic  3.6 us (1%)
  local copies, waits for them, and re-layouts  3.58 us (1%)
    pallas_call x1, Pallas kernels, opening(): pl.pallas_call(functools.partial(opening_body, n, wq.shape[0]), in_specs=...  74.7 us
    pallas_call x1, Pallas kernels, descend(): pl.pallas_call(functools.partial(descend_body, n), in_specs=[vmem, pl.Blo...  62.5 us
    pallas_call x2, Pallas kernels, finish(): pl.pallas_call(functools.partial(finish_body, n, active, wq.shape[0]), in...  57.6 us
    pallas_call x2, Pallas kernels, attend(): pl.pallas_call(functools.partial(attend_body, n, active, gather), in_spec...  33.4 us

profile of v5, /device:TPU:0, one launch (start us, length us, event | category | flops | bytes accessed | tf_op | source)
XLA Modules:
  0.0 239.8 jit_solution(14262691242963653690)
XLA Ops:
  0.0 1.3 constant_dynamic-slice_fusion.gain_ref
  1.3 0.2 multiply_cosine_fusion
  1.5 0.1 pad_maximum_fusion.2.cos_ref
  1.6 0.0 copy-start.1
  1.6 0.1 pad_maximum_fusion.3.sin_ref
  1.7 0.0 copy-start.2
  1.8 2.2 convolution_convert_fusion
  4.0 0.0 copy-start.3
  4.0 74.7 %shard_map.91 = (f32[128,2048]{1,0:T(8,128)}, f32[128,512]{1,0:T(8,128)}, f32[128,128]{1,0:T(8,128)}, bf16[64,2048]{1,0:T(8,128)(2,1)}) custom-call(bf16[128,2048]{1,0:T(8,128)(2,1)} %bitcast.39, bf16[64,2048]{1,0:T(8,128)(2,1)} %bitcast.46, bf16[2048,2048]{1,0:T(8,128)(2,1)} %bitcast.37, f32[4,1,2048]{2,1,0:T(1,128)} %bitcast.58, ...), custom_call_target="tpu_custom_call" | custom-call | tf_op jit(solution)/shard_map/pallas_call | solution.py:254
  78.6 0.0 copy-done.1
  78.7 0.0 copy-done.2
  78.7 0.9 slice.21
  79.6 0.9 slice.13
  80.5 0.1 reshape.69
  80.6 0.2 fusion.8
  80.8 0.2 pad_maximum_fusion
  81.0 0.1 concatenate.17
  81.1 0.7 pad_maximum_fusion.1.kv_ref
  81.8 0.0 copy-done.3
  81.8 2.2 convolution_convert_fusion.1.o_ref
  84.0 15.7 %shard_map.92 = (bf16[2,64,2048]{2,1,0:T(8,128)(2,1)}, bf16[2,64,512]{2,1,0:T(8,128)(2,1)}, bf16[4,2,64,512]{3,2,1,0:T(8,128)(2,1)}) custom-call(s32[2]{0:T(128)} %lens_ref.3, f32[2,64,2048]{2,1,0:T(8,128)} %bitcast.42, bf16[2,64,2048]{2,1,0:T(8,128)(2,1)} %convolution_convert_fusion.1.o_ref, bf16[2,64,512]{2,1,0:T(8,128)(2,1)} %pad_maximum_fusion.1.kv_ref, ...), custom_call_target="tpu_custom_call" | custom-call | tf_op jit(solution)/shard_map/pallas_call | solution.py:724
  99.6 13.9 %shard_map.93 = (f32[128,2048]{1,0:T(8,128)}, bf16[128,2048]{1,0:T(8,128)(2,1)}) custom-call(bf16[128,2048]{1,0:T(8,128)(2,1)} %bitcast.48, bf16[128,512]{1,0:T(8,128)(2,1)} %bitcast.57, bf16[128,2048]{1,0:T(8,128)(2,1)} %bitcast.40, bf16[128,2048]{1,0:T(8,128)(2,1)} %bitcast.44, f32[1,2048]{1,0:T(1,128)} %constant_dynamic-slice_fusion.gain_ref, ...), custom_call_target="tpu_custom_call" | custom-call | tf_op jit(solution)/shard_map/pallas_call | solution.py:428
  113.6 62.5 %shard_map.94 = (bf16[128,2048]{1,0:T(8,128)(2,1)}, bf16[128,2048]{1,0:T(8,128)(2,1)}) custom-call(bf16[128,2048]{1,0:T(8,128)(2,1)} %get-tuple-element.25.g_ref, bf16[2048,2048]{1,0:T(8,128)(2,1)} %bitcast.38), custom_call_target="tpu_custom_call" | custom-call | tf_op jit(solution)/shard_map/pallas_call | solution.py:563
  176.0 17.8 %shard_map.95 = (bf16[2,64,2048]{2,1,0:T(8,128)(2,1)}, bf16[2,64,512]{2,1,0:T(8,128)(2,1)}) custom-call(s32[2]{0:T(128)} %lens_ref.3, f32[2,64,2048]{2,1,0:T(8,128)} %bitcast.43, bf16[2,64,2048]{2,1,0:T(8,128)(2,1)} %bitcast.49, bf16[4,2,64,512]{3,2,1,0:T(8,128)(2,1)} %get-tuple-element.27.kv_ref, f32[64,128]{1,0:T(8,128)} %copy-done.1, f32[64,128]{1,0:T(8,128)} %copy-done.2), custom_call_target="tpu_custom_call" | custom-call | tf_op jit(solution)/shard_map/pallas_call | solution.py:724
  193.8 0.0 copy-start
  193.8 43.6 %shard_map.96 = (f32[128,2048]{1,0:T(8,128)}, bf16[128,2048]{1,0:T(8,128)(2,1)}) custom-call(bf16[128,2048]{1,0:T(8,128)(2,1)} %bitcast.47, bf16[128,512]{1,0:T(8,128)(2,1)} %bitcast.56, bf16[128,2048]{1,0:T(8,128)(2,1)} %bitcast.41, bf16[128,2048]{1,0:T(8,128)(2,1)} %get-tuple-element.30.up_ref, f32[1,2048]{1,0:T(1,128)} %constant_dynamic-slice_fusion.gain_ref, ...), custom_call_target="tpu_custom_call" | custom-call | tf_op jit(solution)/shard_map/pallas_call | solution.py:428
  237.5 0.0 copy-done
  237.5 2.3 broadcast_select_fusion
  (7 shorter events, 0.1 us)
Async XLA Ops:
  1.6 77.1 %copy-start.1 = (f32[64,128]{1,0:T(8,128)}, f32[64,128]{1,0:T(8,128)S(1)}, u32[]{:S(2)}) copy-start(f32[64,128]{1,0:T(8,128)S(1)} %pad_maximum_fusion.2.cos_ref) | copy-start | bytes 98308
  1.7 77.0 %copy-start.2 = (f32[64,128]{1,0:T(8,128)}, f32[64,128]{1,0:T(8,128)S(1)}, u32[]{:S(2)}) copy-start(f32[64,128]{1,0:T(8,128)S(1)} %pad_maximum_fusion.3.sin_ref) | copy-start | bytes 98308
  4.0 77.8 %copy-start.3 = (s32[2,32]{1,0:T(2,128)S(1)}, s32[2,32]{1,0:T(2,128)}, u32[]{:S(2)}) copy-start(s32[2,32]{1,0:T(2,128)} %param.11) | copy-start | bytes 772
  193.8 43.7 %copy-start = (f32[128,2048]{1,0:T(8,128)S(1)}, f32[128,2048]{1,0:T(8,128)}, u32[]{:S(2)}) copy-start(f32[128,2048]{1,0:T(8,128)} %get-tuple-element.32) | copy-start | bytes 3145732
